TPU v7x, 512 devices: a whole 4x8x8 slice. The times are simulated.
512 devices in a mesh: narrow: 16 (over x, y_hi, core), wide: 32 (over y_lo, z).
Axes of the slice: x: 4, y: 8 (y_hi: 2, y_lo: 4; y = y_hi * 4 + y_lo), z: 8, core: 2. Of those that a mesh axis runs over, the one named last changes fastest.
Arguments:
- inputs: bfloat16 [128, 2304], P('wide', 'narrow'), may hold values from -6 to 6
- decoder_bias: float32 [2304], replicated, may hold values from -3 to 3
- preactivations: bfloat16 [128, 131072], P(None, ('narrow', 'wide')), may hold values from -6 to 6
- decoder_weight: bfloat16 [131072, 2304], P(('narrow', 'wide')), may hold values from -0.0625 to 0.0625
Outputs:
- grad_encoder: bfloat16 [2304, 131072], P(None, ('narrow', 'wide'))
- grad_decoder: bfloat16 [131072, 2304], P(('narrow', 'wide'))
All inputs are finite; a program needn't handle non-finite values.
Results may differ from a plain program's by a relative error of at most 0.0053.
Values may be sent and summed in bfloat16 or wider, within the bound.
No kernel may reach another device: no remote copies, remote signals or barrier semaphores. Data moves between devices by JAX's collectives and lax.ppermute only.
A program may use at most 64 MiB of HBM per device.

v0:
```python
import jax
import jax.numpy as jnp
from jax import lax
from jax.sharding import PartitionSpec as P


def laid_out(pieces, dim):
    dims = list(pieces.shape[1:])
    dims[dim] *= pieces.shape[0]
    return jnp.moveaxis(pieces, 0, dim).reshape(dims)


def from_everyone(x, axis):
    length = lax.axis_size(axis)
    return lax.all_to_all(jnp.broadcast_to(x[None], (length, *x.shape)), axis, 0, 0, tiled=True)


def gather_directly(x, axis, dim):
    return laid_out(from_everyone(x, axis), dim)


def in_blocks(x, dim, length):
    before, after = (x.shape[:dim], x.shape[dim + 1 :])
    return jnp.moveaxis(x.reshape(*before, length, -1, *after), dim, 0)


def sum_at_owner(x, axis, dim):
    pieces = in_blocks(x, dim, lax.axis_size(axis))
    arrived = lax.all_to_all(pieces, axis, split_axis=0, concat_axis=0, tiled=True)
    return arrived.sum(axis=0)


def shards(inputs, decoder_bias, preactivations, decoder_weight):
    halfway = gather_directly(inputs, "wide", 0)
    gathered = lax.all_gather(halfway, "narrow", axis=1, tiled=True)
    centered = (gathered.astype(jnp.float32) - decoder_bias).astype(jnp.bfloat16)
    hidden = jnp.maximum(preactivations, jnp.zeros_like(preactivations))
    partial_value = jnp.dot(hidden, decoder_weight, preferred_element_type=jnp.float32)
    reduced = sum_at_owner(partial_value, "wide", 0)
    reduced = sum_at_owner(reduced, "narrow", 1)
    columns = inputs.shape[1]
    bias_cols = lax.dynamic_slice_in_dim(decoder_bias, lax.axis_index("narrow") * columns, columns)
    residual = (reduced + bias_cols - inputs.astype(jnp.float32)).astype(jnp.bfloat16)
    resid_half = gather_directly(residual, "wide", 0)
    resid_whole = gather_directly(resid_half, "narrow", 1)
    grad_decoder = jnp.einsum(
        "bf,bd->fd", hidden, resid_whole, preferred_element_type=jnp.float32
    ).astype(jnp.bfloat16)
    backward = jnp.einsum(
        "bd,fd->bf", resid_whole, decoder_weight, preferred_element_type=jnp.float32
    )
    masked = jnp.where(preactivations > 0, backward, jnp.zeros_like(backward)).astype(jnp.bfloat16)
    grad_encoder = jnp.einsum(
        "bd,bf->df", centered, masked, preferred_element_type=jnp.float32
    ).astype(jnp.bfloat16)
    return (grad_encoder, grad_decoder)


def solution(mesh):
    placed = (P("wide", "narrow"), P(), P(None, ("narrow", "wide")), P(("narrow", "wide"), None))
    return jax.shard_map(
        shards,
        mesh=mesh,
        in_specs=placed,
        out_specs=(P(None, ("narrow", "wide")), P(("narrow", "wide"), None)),
        check_vma=False,
    )
```

profile of v0, /device:TPU:41, one launch (start us, length us, event | category | flops | bytes accessed | tf_op | source)
XLA Modules:
  0.0 147.5 jit_solution(8714161629953091175)
XLA Ops:
  0.6 0.0 copy-start
  0.6 1.3 copy-done
  1.9 1.2 fusion.5
  3.1 0.3 reshape.22
  3.4 42.4 %all_to_all.25 = f32[32,4,2304]{2,1,0:T(4,128)S(1)} all-to-all(f32[32,4,2304]{2,1,0:T(4,128)S(1)} %reshape.22), channel_id=1, replica_groups=mesh['narrow'=16,'wide'=32] {'wide'}, dimensions={0} | all-to-all | bytes 2359296 | tf_op jit(solution)/shard_map/all_to_all | solution.py:29
  45.8 0.0 copy-start.2
  45.9 0.0 copy-start.3
  45.9 0.2 reduce_sum.18
  46.0 0.1 reshape.23
  46.1 0.7 copy.10
  46.8 11.4 %all-to-all-start.2 = ((f32[16,4,144]{2,1,0:T(4,128)}), f32[16,4,144]{2,1,0:T(4,128)S(1)}, u32[]{:S(2)}, u32[]{:S(2)}) async-start(f32[16,4,144]{2,1,0:T(4,128)} %copy.10), calls=%async_computation.2 | async-start | bytes 131072 | tf_op jit(solution)/shard_map/all_to_all | solution.py:29
  58.2 0.0 copy-done.2
  58.2 0.1 dynamic_slice.3
  58.3 5.2 %all-to-all-done.2 = f32[16,4,144]{2,1,0:T(4,128)S(1)} async-done(((f32[16,4,144]{2,1,0:T(4,128)}), f32[16,4,144]{2,1,0:T(4,128)S(1)}, u32[]{:S(2)}, u32[]{:S(2)}) %all-to-all-start.2) | async-done | bytes 36896 | tf_op jit(solution)/shard_map/all_to_all | solution.py:29
  63.5 0.0 copy-done.3
  63.6 12.0 %all_to_all.26 = bf16[32,4,144]{2,1,0:T(4,128)(2,1)S(1)} all-to-all(bf16[32,4,144]{2,1,0:T(4,128)(2,1)S(1)} %broadcast_in_dim.11), channel_id=1, replica_groups=mesh['narrow'=16,'wide'=32] {'wide'}, dimensions={0} | all-to-all | bytes 73728 | tf_op jit(solution)/shard_map/all_to_all | solution.py:15
  75.6 0.6 broadcast_in_dim.10
  76.3 4.7 %all-to-all-start = ((bf16[32,4,144]{2,1,0:T(4,128)(2,1)}), bf16[32,4,144]{2,1,0:T(4,128)(2,1)S(1)}, u32[]{:S(2)}, u32[]{:S(2)}) async-start(bf16[32,4,144]{2,1,0:T(4,128)(2,1)} %broadcast_in_dim.10), calls=%async_computation | async-start | bytes 131072 | tf_op jit(solution)/shard_map/all_to_all | solution.py:15
  81.0 0.1 copy.11
  81.1 0.0 copy-start.1
  81.1 8.1 %all-to-all-done = bf16[32,4,144]{2,1,0:T(4,128)(2,1)S(1)} async-done(((bf16[32,4,144]{2,1,0:T(4,128)(2,1)}), bf16[32,4,144]{2,1,0:T(4,128)(2,1)S(1)}, u32[]{:S(2)}, u32[]{:S(2)}) %all-to-all-start) | async-done | bytes 36896 | tf_op jit(solution)/shard_map/all_to_all | solution.py:15
  89.3 0.9 broadcast_in_dim.13
  90.2 11.2 %all-to-all-start.4 = ((bf16[16,128,144]{1,2,0:T(8,128)(2,1)}), bf16[16,128,144]{1,2,0:T(8,128)(2,1)S(1)}, u32[]{:S(2)}, u32[]{:S(2)}) async-start(bf16[16,128,144]{1,2,0:T(8,128)(2,1)} %broadcast_in_dim.13), calls=%async_computation.4 | async-start | bytes 1179648 | tf_op jit(solution)/shard_map/all_to_all | solution.py:15
  101.5 0.1 copy.9
  101.6 41.9 %all_gather.3 = bf16[128,2304]{0,1:T(8,128)(2,1)S(1)} all-gather(bf16[128,144]{0,1:T(8,128)(2,1)S(1)} %copy.9), channel_id=1, replica_groups=mesh['narrow'=16,'wide'=32] {'narrow'}, dimensions={1}, use_global_device_ids=true | all-gather | bytes 626688 | tf_op jit(solution)/shard_map/all_gather | solution.py:35
  143.4 0.0 all-to-all-done.4
  143.4 0.0 copy-done.1
  143.4 1.5 %convolution_convert_fusion = bf16[256,2304]{1,0:T(8,128)(2,1)} fusion(bf16[128,2304]{0,1:T(8,128)(2,1)S(1)} %bitcast.8, bf16[128,256]{1,0:T(8,128)(2,1)S(1)} %copy-done.1), kind=kOutput, calls=%fused_computation | convolution fusion | flops 151617536 | bytes 1835008 | tf_op jit(solution)/shard_map/bf,bd->fd/dot_general | solution.py:46
  145.0 2.5 %convolution_convert_fusion.1 = bf16[2304,256]{1,0:T(8,128)(2,1)} fusion(bf16[128,2304]{0,1:T(8,128)(2,1)S(1)} %bitcast.9, bf16[256,2304]{1,0:T(8,128)(2,1)S(1)} %copy-done, bf16[128,2304]{0,1:T(8,128)(2,1)S(1)} %all_gather.3, f32[2304]{0:T(1024)S(1)} %copy-done.2, bf16[128,256]{1,0:T(8,128)(2,1)S(1)} %copy-done.1), kind=kOutput, calls=%fused_computation.1 | convolution fusion | flops 303562752 | bytes 3613696 | tf_op jit(solution)/shard_map/bd,bf->df/dot_general | solution.py:53
  (5 shorter events, 0.1 us)
Async XLA Ops:
  0.6 1.3 copy-start
  45.8 12.3 %copy-start.2 = (f32[2304]{0:T(1024)S(1)}, f32[2304]{0:T(1024)}, u32[]{:S(2)}) copy-start(f32[2304]{0:T(1024)} %param.5) | copy-start | bytes 27652
  45.9 17.7 %copy-start.3 = (bf16[4,144]{1,0:T(4,128)(2,1)S(1)}, bf16[4,144]{1,0:T(4,128)(2,1)}, u32[]{:S(2)}) copy-start(bf16[4,144]{1,0:T(4,128)(2,1)} %param.4) | copy-start | bytes 3460
  46.8 16.7 %all-to-all-start.2 = ((f32[16,4,144]{2,1,0:T(4,128)}), f32[16,4,144]{2,1,0:T(4,128)S(1)}, u32[]{:S(2)}, u32[]{:S(2)}) async-start(f32[16,4,144]{2,1,0:T(4,128)} %copy.10), calls=%async_computation.2 | async-start | bytes 131072 | tf_op jit(solution)/shard_map/all_to_all | solution.py:29
  76.3 13.0 %all-to-all-start = ((bf16[32,4,144]{2,1,0:T(4,128)(2,1)}), bf16[32,4,144]{2,1,0:T(4,128)(2,1)S(1)}, u32[]{:S(2)}, u32[]{:S(2)}) async-start(bf16[32,4,144]{2,1,0:T(4,128)(2,1)} %broadcast_in_dim.10), calls=%async_computation | async-start | bytes 131072 | tf_op jit(solution)/shard_map/all_to_all | solution.py:15
  81.1 62.3 %copy-start.1 = (bf16[128,256]{1,0:T(8,128)(2,1)S(1)}, bf16[128,256]{1,0:T(8,128)(2,1)}, u32[]{:S(2)}) copy-start(bf16[128,256]{1,0:T(8,128)(2,1)} %param.6) | copy-start | bytes 196612
  90.2 53.3 %all-to-all-start.4 = ((bf16[16,128,144]{1,2,0:T(8,128)(2,1)}), bf16[16,128,144]{1,2,0:T(8,128)(2,1)S(1)}, u32[]{:S(2)}, u32[]{:S(2)}) async-start(bf16[16,128,144]{1,2,0:T(8,128)(2,1)} %broadcast_in_dim.13), calls=%async_computation.4 | async-start | bytes 1179648 | tf_op jit(solution)/shard_map/all_to_all | solution.py:15
where the time goes:
time: 148 us; the launch traced here: 147 us
  blocking collectives  96.3 us (65%)
  starting transfers between devices  27.3 us (18%)
  waiting for transfers between devices  13.4 us (9%)
  matrix products  5.2 us (4%)
  local copies, waits for them, and re-layouts  4.33 us (3%)
    all_to_all x1, blocking collectives, sum_at_owner(): lax.all_to_all(pieces, axis, split_axis=0, concat_axis=0, tiled=True)  42.4 us
    all_gather x1, blocking collectives, shards(): gathered = lax.all_gather(halfway, 'narrow', axis=1, tiled=True)  41.9 us
    all_to_all x2, starting transfers between devices, from_everyone(): lax.all_to_all(jnp.broadcast_to(x[None], (length, *x.shape)), axis, 0, 0,...  15.9 us
    all_to_all x1, blocking collectives, from_everyone(): lax.all_to_all(jnp.broadcast_to(x[None], (length, *x.shape)), axis, 0, 0,...  12 us
    all_to_all x1, starting transfers between devices, sum_at_owner(): lax.all_to_all(pieces, axis, split_axis=0, concat_axis=0, tiled=True)  11.4 us
    all_to_all x2, waiting for transfers between devices, from_everyone(): lax.all_to_all(jnp.broadcast_to(x[None], (length, *x.shape)), axis, 0, 0,...  8.14 us
    all_to_all x1, waiting for transfers between devices, sum_at_owner(): lax.all_to_all(pieces, axis, split_axis=0, concat_axis=0, tiled=True)  5.21 us
  transfers between devices with their start and end apart: 3, of which 2 were waited for; matrix products, arithmetic and copies ran while one was open for 0% of the time, Pallas kernels for 0%

commit v1 on v0

v1 whole, which is shorter than its diff:
```python
import jax
import jax.numpy as jnp
from jax import lax
from jax.sharding import Mesh, PartitionSpec as P


def swap(x, axis):
    return lax.all_to_all(x, axis, split_axis=0, concat_axis=0, tiled=True)


def to_all(x, axis):
    return swap(jnp.broadcast_to(x[None], (lax.axis_size(axis), *x.shape)), axis)


def shards(inputs, decoder_bias, preactivations, decoder_weight):
    rows, columns = inputs.shape
    narrow = ("pair", "core")
    wide, pairs, cores = (lax.axis_size(a) for a in ("wide", "pair", "core"))
    width = decoder_weight.shape[1]
    half = width // cores
    core = lax.axis_index("core")

    hidden = jnp.maximum(preactivations, jnp.zeros_like(preactivations))
    partial_sum = jnp.dot(hidden, decoder_weight, preferred_element_type=jnp.float32)
    arrived = swap(partial_sum.astype(jnp.bfloat16).reshape(wide, rows, width), "wide")
    mine = arrived.astype(jnp.float32).sum(axis=0).astype(jnp.bfloat16)

    halves = jnp.moveaxis(mine.reshape(rows, cores, half), 1, 0)
    halves = jnp.broadcast_to(halves[None], (pairs, cores, rows, half)).reshape(-1, rows, half)
    block = jnp.broadcast_to(inputs[None], (pairs * cores, rows, columns))
    arrived = swap(jnp.concatenate([halves, block], axis=2), narrow)
    reduced = arrived[:, :, :half].astype(jnp.float32).sum(axis=0)
    whole_rows = jnp.moveaxis(arrived[:, :, half:], 0, 1).reshape(rows, width)
    my_inputs = lax.dynamic_slice_in_dim(whole_rows, core * half, half, 1).astype(jnp.float32)
    my_bias = lax.dynamic_slice_in_dim(decoder_bias, core * half, half)
    residual = (reduced + my_bias - my_inputs).astype(jnp.bfloat16)
    centered = (my_inputs - my_bias).astype(jnp.bfloat16)

    gathered = to_all(jnp.stack([residual, centered]), "wide")
    gathered = jnp.moveaxis(gathered, 0, 1).reshape(2, wide * rows, half)
    both = to_all(gathered, "core")
    residual = jnp.concatenate([both[i, 0] for i in range(cores)], axis=1)
    centered = jnp.concatenate([both[i, 1] for i in range(cores)], axis=1)

    grad_decoder = jnp.einsum(
        "bf,bd->fd", hidden, residual, preferred_element_type=jnp.float32
    ).astype(jnp.bfloat16)
    backward = jnp.einsum("bd,fd->bf", residual, decoder_weight, preferred_element_type=jnp.float32)
    masked = jnp.where(preactivations > 0, backward, jnp.zeros_like(backward)).astype(jnp.bfloat16)
    grad_encoder = jnp.einsum(
        "bd,bf->df", centered, masked, preferred_element_type=jnp.float32
    ).astype(jnp.bfloat16)
    return (grad_encoder, grad_decoder)


def solution(mesh):
    narrow, wide = (mesh.shape[a] for a in ("narrow", "wide"))
    split = Mesh(mesh.devices.reshape(narrow // 2, 2, wide), ("pair", "core", "wide"))
    columns = ("pair", "core")
    features = ("pair", "core", "wide")
    return jax.shard_map(
        shards,
        mesh=split,
        in_specs=(P("wide", columns), P(), P(None, features), P(features, None)),
        out_specs=(P(None, features), P(features, None)),
        check_vma=False,
    )
```

time: 148 us -> 90.1 us (0.61)
  the two profiles are of different devices: /device:TPU:41 before, /device:TPU:1 now
where the time goes in v1:
time: 90.1 us; the launch traced here: 89.7 us
  blocking collectives  59.6 us (66%)
  waiting for transfers between devices  10.4 us (12%)
  starting transfers between devices  9.57 us (11%)
  matrix products  5.19 us (6%)
  local copies, waits for them, and re-layouts  2.99 us (3%)
  other arithmetic  1.12 us (1%)
    all_to_all x3, blocking collectives, swap(): return lax.all_to_all(x, axis, split_axis=0, concat_axis=0, tiled=True)  59.6 us
    all_to_all x1, waiting for transfers between devices, swap(): return lax.all_to_all(x, axis, split_axis=0, concat_axis=0, tiled=True)  10.4 us
    all_to_all x1, starting transfers between devices, swap(): return lax.all_to_all(x, axis, split_axis=0, concat_axis=0, tiled=True)  9.57 us
    dot_general x1, matrix products, shards(): jnp.einsum('bd,bf->df', centered, masked, preferred_element_type=jnp.floa...  2.52 us
    unnamed x8, local copies, waits for them, and re-layouts  2.02 us
  transfers between devices with their start and end apart: 1, of which 1 were waited for; matrix products, arithmetic and copies ran while one was open for 0% of the time, Pallas kernels for 0%

profile of v1, /device:TPU:1, one launch (start us, length us, event | category | flops | bytes accessed | tf_op | source)
XLA Modules:
  0.0 89.7 jit_solution(13553104010566432486)
XLA Ops:
  0.6 0.0 copy-start
  0.6 1.3 %copy-done = bf16[256,2304]{1,0:T(8,128)(2,1)S(1)} copy-done((bf16[256,2304]{1,0:T(8,128)(2,1)S(1)}, bf16[256,2304]{1,0:T(8,128)(2,1)}, u32[]{:S(2)}) %copy-start) | copy-done | bytes 1179672
  1.9 1.2 %convolution_convert_fusion.2 = bf16[128,2304]{1,0:T(8,128)(2,1)S(1)} fusion(bf16[256,2304]{1,0:T(8,128)(2,1)S(1)} %copy-done, bf16[128,256]{1,0:T(8,128)(2,1)} %param.6), kind=kOutput, calls=%fused_computation.2 | convolution fusion | flops 151322624 | bytes 1835008 | tf_op jit(solution)/shard_map/dot_general | solution.py:24
  3.1 0.1 reshape.21
  3.2 0.0 copy-start.3
  3.2 0.0 copy-start.2
  3.2 30.2 %all_to_all.20 = bf16[32,4,2304]{2,1,0:T(4,128)(2,1)S(1)} all-to-all(bf16[32,4,2304]{2,1,0:T(4,128)(2,1)S(1)} %reshape.21), channel_id=1, replica_groups=mesh['pair'=8,'core'=2,'wide'=32] {'wide'}, dimensions={0} | all-to-all | bytes 1179648 | tf_op jit(solution)/shard_map/all_to_all | solution.py:8
  33.5 0.3 reduce_sum.21
  33.7 0.0 copy-done.3
  33.8 0.8 pad_maximum_fusion.4
  34.5 9.6 %all-to-all-start.1 = ((bf16[16,4,1296]{2,1,0:T(4,128)(2,1)}), bf16[16,4,1296]{2,1,0:T(4,128)(2,1)S(1)}, u32[]{:S(2)}, u32[]{:S(2)}) async-start(bf16[16,4,1296]{2,1,0:T(4,128)(2,1)} %pad_maximum_fusion.4), calls=%async_computation.1 | async-start | bytes 360448 | tf_op jit(solution)/shard_map/all_to_all | solution.py:8
  44.1 0.0 copy-done.2
  44.1 0.1 dynamic_slice.6
  44.2 10.4 %all-to-all-done.1 = bf16[16,4,1296]{2,1,0:T(4,128)(2,1)S(1)} async-done(((bf16[16,4,1296]{2,1,0:T(4,128)(2,1)}), bf16[16,4,1296]{2,1,0:T(4,128)(2,1)S(1)}, u32[]{:S(2)}, u32[]{:S(2)}) %all-to-all-start.1) | async-done | bytes 165920 | tf_op jit(solution)/shard_map/all_to_all | solution.py:8
  54.7 0.1 reshape.24
  54.8 0.1 convert_reduce_fusion
  54.9 0.3 broadcast_in_dim.14
  55.3 22.6 %all_to_all.21 = bf16[32,2,4,1152]{3,1,2,0:T(2,128)(2,1)S(1)} all-to-all(bf16[32,2,4,1152]{3,1,2,0:T(2,128)(2,1)S(1)} %broadcast_in_dim.14), channel_id=1, replica_groups=mesh['pair'=8,'core'=2,'wide'=32] {'wide'}, dimensions={0} | all-to-all | bytes 1179648 | tf_op jit(solution)/shard_map/all_to_all | solution.py:8
  77.8 0.1 copy.11
  77.9 0.1 broadcast_in_dim.16
  78.0 6.8 %all_to_all.22 = bf16[2,2,128,1152]{3,2,1,0:T(8,128)(2,1)S(1)} all-to-all(bf16[2,2,128,1152]{3,2,1,0:T(8,128)(2,1)S(1)} %broadcast_in_dim.16), channel_id=1, replica_groups=mesh['pair'=8,'core'=2,'wide'=32] {'core'}, dimensions={0} | all-to-all | bytes 2359296 | tf_op jit(solution)/shard_map/all_to_all | solution.py:8
  84.8 0.0 copy-start.1
  84.8 0.1 slice_bitcast_fusion.1
  84.9 0.7 copy-done.1
  85.7 1.5 %convolution_convert_fusion = bf16[256,2304]{1,0:T(8,128)(2,1)} fusion(bf16[128,1152]{1,0:T(8,128)(2,1)S(1)} %get-tuple-element.3, bf16[128,1152]{1,0:T(8,128)(2,1)S(1)} %get-tuple-element.2, bf16[128,256]{1,0:T(8,128)(2,1)S(1)} %copy-done.1), kind=kOutput, calls=%fused_computation | convolution fusion | flops 152797184 | bytes 1835008 | tf_op jit(solution)/shard_map/bf,bd->fd/dot_general | solution.py:45
  87.2 2.5 %convolution_convert_fusion.1 = bf16[2304,256]{1,0:T(8,128)(2,1)} fusion(bf16[256,2304]{1,0:T(8,128)(2,1)S(1)} %copy-done, bf16[128,1152]{1,0:T(8,128)(2,1)S(1)} %get-tuple-element.4, bf16[128,1152]{1,0:T(8,128)(2,1)S(1)} %get-tuple-element.5, bf16[128,1152]{1,0:T(8,128)(2,1)S(1)} %get-tuple-element.3, bf16[128,1152]{1,0:T(8,128)(2,1)S(1)} %get-tuple-element.2, ...), kind=kOutput, calls=%fused_computation.1 | convolution fusion | flops 305037312 | bytes 3604480 | tf_op jit(solution)/shard_map/bd,bf->df/dot_general | solution.py:50
  (7 shorter events, 0.1 us)
Async XLA Ops:
  0.6 1.3 %copy-start = (bf16[256,2304]{1,0:T(8,128)(2,1)S(1)}, bf16[256,2304]{1,0:T(8,128)(2,1)}, u32[]{:S(2)}) copy-start(bf16[256,2304]{1,0:T(8,128)(2,1)} %param.7) | copy-start | bytes 3538948
  3.2 30.5 %copy-start.3 = (bf16[4,144]{1,0:T(4,128)(2,1)S(1)}, bf16[4,144]{1,0:T(4,128)(2,1)}, u32[]{:S(2)}) copy-start(bf16[4,144]{1,0:T(4,128)(2,1)} %param.4) | copy-start | bytes 3460
  3.2 40.9 %copy-start.2 = (f32[2304]{0:T(1024)S(1)}, f32[2304]{0:T(1024)}, u32[]{:S(2)}) copy-start(f32[2304]{0:T(1024)} %param.5) | copy-start | bytes 27652
  34.5 20.1 %all-to-all-start.1 = ((bf16[16,4,1296]{2,1,0:T(4,128)(2,1)}), bf16[16,4,1296]{2,1,0:T(4,128)(2,1)S(1)}, u32[]{:S(2)}, u32[]{:S(2)}) async-start(bf16[16,4,1296]{2,1,0:T(4,128)(2,1)} %pad_maximum_fusion.4), calls=%async_computation.1 | async-start | bytes 360448 | tf_op jit(solution)/shard_map/all_to_all | solution.py:8
  84.8 0.8 copy-start.1

commit v2 on v1

v2 whole, which is shorter than its diff:
```python
import jax
import jax.numpy as jnp
from jax import lax
from jax.experimental import pallas as pl
from jax.experimental.pallas import tpu as pltpu
from jax.sharding import Mesh, PartitionSpec as P

BF16, F32 = jnp.bfloat16, jnp.float32
LANES = 128


def swap(x, axis):
    return lax.all_to_all(x, axis, split_axis=0, concat_axis=0, tiled=True)


def to_all(x, axis):
    return swap(jnp.broadcast_to(x[None], (lax.axis_size(axis), *x.shape)), axis)


def dot(a, b, contract):
    return lax.dot_general(a, b, ((contract[:1], contract[1:]), ((), ())), preferred_element_type=F32)


def first_kernel(pre, weight, extra, out):
    hidden = jnp.maximum(pre[...], jnp.zeros_like(pre[...]))
    rows = hidden.shape[0]
    out[0, :rows, :] = dot(hidden, weight[...], (1, 0)).astype(BF16)
    out[0, rows:, :] = extra[...]


def first_product(pre, weight, extra):
    rows, features = pre.shape
    half = weight.shape[1] // 2
    more = extra.shape[0]
    return pl.pallas_call(
        first_kernel,
        grid=(2,),
        out_shape=jax.ShapeDtypeStruct((2, rows + more, half), BF16),
        in_specs=[
            pl.BlockSpec((rows, features), lambda i: (0, 0)),
            pl.BlockSpec((features, half), lambda i: (0, i)),
            pl.BlockSpec((more, half), lambda i: (0, 0)),
        ],
        out_specs=pl.BlockSpec((1, rows + more, half), lambda i: (i, 0, 0)),
        name="first_product",
    )(pre, weight, extra)


def last_kernel(both, pre, weight, decoder_out, encoder_out, decoder, encoder, sems):
    cores, rows, _ = both.shape
    features = pre.shape[1]
    half = weight.shape[1] // cores
    hidden = jnp.maximum(pre[...], jnp.zeros_like(pre[...]))
    copies = []

    def send(source, target):
        copies.append(pltpu.make_async_copy(source, target, sems.at[len(copies)]))
        copies[-1].start()

    backward = jnp.zeros((rows, features), F32)
    for c in range(cores):
        residual = both[c, :, :half]
        columns = pl.ds(c * half, half)
        decoder[c] = dot(hidden, residual, (0, 0)).astype(BF16)
        send(decoder.at[c], decoder_out.at[:, columns])
        backward += dot(residual, weight[:, columns], (1, 1))
    masked = jnp.where(pre[...] > 0, backward, jnp.zeros_like(backward)).astype(BF16)
    blocks, width = encoder.shape[:2]
    depth = rows // blocks
    padded = -(-width // LANES) * LANES
    for x in range(blocks):
        part = [
            both[c, x * depth : (x + 1) * depth, half + h * padded : half + (h + 1) * padded]
            for c in range(cores)
            for h in range(blocks // cores)
        ]
        product = dot(jnp.concatenate(part, axis=0), masked, (0, 0))
        encoder[x] = product[:width].astype(BF16)
        send(encoder.at[x], encoder_out.at[pl.ds(x * width, width), :])
    for copy in copies:
        copy.wait()


def last_products(both, pre, weight, blocks):
    cores = both.shape[0]
    features, width = weight.shape
    return pl.pallas_call(
        last_kernel,
        out_shape=(
            jax.ShapeDtypeStruct((features, width), BF16),
            jax.ShapeDtypeStruct((width, features), BF16),
        ),
        in_specs=[pl.BlockSpec(memory_space=pltpu.VMEM)] * 3,
        out_specs=(pl.BlockSpec(memory_space=pl.ANY),) * 2,
        scratch_shapes=[
            pltpu.VMEM((cores, features, width // cores), BF16),
            pltpu.VMEM((blocks, width // blocks, features), BF16),
            pltpu.SemaphoreType.DMA((cores + blocks,)),
        ],
        compiler_params=pltpu.CompilerParams(vmem_limit_bytes=16 << 20),
        name="last_products",
    )(both, pre, weight)


def shards(inputs, decoder_bias, preactivations, decoder_weight):
    rows, columns = inputs.shape
    width = decoder_weight.shape[1]
    xs, yhs, cores, yls, zs = (lax.axis_size(a) for a in ("x", "yh", "core", "yl", "z"))
    x, yh, core, yl, z = (lax.axis_index(a) for a in ("x", "yh", "core", "yl", "z"))
    half, quarter, pair = width // cores, width // xs, columns * cores
    pieces = xs * zs

    extra = jnp.pad(inputs, ((0, 16 - rows), (0, half - columns)))
    arrived = swap(first_product(preactivations, decoder_weight, extra), "core")
    batch = preactivations.shape[0]
    blocks = arrived[:, batch : batch + rows, :columns]
    block = jnp.concatenate([blocks[c] for c in range(cores)], axis=1)
    strip = lax.dynamic_update_slice_in_dim(
        jnp.zeros((rows, half), BF16), block, (x * quarter) % half + yh * pair, 1
    ).astype(F32)
    owner = jnp.where((x * quarter) // half == core, yl * zs + z, pieces)
    whole = arrived[:, :batch].reshape(cores, pieces, rows, half).astype(F32)
    mine = lax.broadcasted_iota(jnp.int32, (pieces, 1, 1), 0) == owner
    partial_sum = whole[0] + whole[1] - jnp.where(mine, strip[None], jnp.zeros_like(strip)[None])

    arrived = swap(partial_sum.astype(BF16), ("x", "z"))
    summed = arrived.astype(F32).sum(axis=0).astype(BF16)
    arrived = to_all(jnp.concatenate([summed, block], axis=1), ("yh", "yl"))
    my_bias = lax.dynamic_slice_in_dim(decoder_bias, core * half, half)
    residual = (arrived[:, :, :half].astype(F32).sum(axis=0) + my_bias).astype(BF16)

    each = yls // cores
    inputs_here = arrived[:, :, half:].reshape(yhs, yls, rows, pair)
    inputs_here = lax.dynamic_slice_in_dim(inputs_here, core * each, each, 1)
    inputs_here = inputs_here.transpose(1, 2, 0, 3).reshape(each, rows, quarter)
    bias_here = lax.dynamic_slice_in_dim(decoder_bias, x * quarter, quarter)
    centered = (inputs_here.astype(F32) - bias_here).astype(BF16)
    spare = -quarter % LANES
    centered = jnp.pad(centered, ((0, 0), (0, 0), (0, spare)))
    payload = jnp.concatenate([residual, *(centered[h] for h in range(each))], axis=1)

    gathered = to_all(payload, ("x", "z")).reshape(batch, -1)
    both = to_all(gathered, "core")
    grad_decoder, grad_encoder = last_products(both, preactivations, decoder_weight, xs)
    return (grad_encoder, grad_decoder)


def solution(mesh):
    split = Mesh(mesh.devices.reshape(4, 2, 2, 4, 8), ("x", "yh", "core", "yl", "z"))
    narrow, wide = ("x", "yh", "core"), ("yl", "z")
    return jax.shard_map(
        shards,
        mesh=split,
        in_specs=(P(wide, narrow), P(), P(None, narrow + wide), P(narrow + wide, None)),
        out_specs=(P(None, narrow + wide), P(narrow + wide, None)),
        check_vma=False,
    )
```

time: 90.1 us -> 85.3 us (0.947)
  blocking collectives: 59.6 us -> 49.1 us
  starting transfers between devices: 9.57 us -> 17.3 us
  matrix products: 5.19 us -> 0 us
  Pallas kernels: 0 us -> 5.02 us
  waiting for transfers between devices: 10.4 us -> 8.88 us
    all_to_all x3, blocking collectives: 59.6 us -> 49.1 us  [swap(): return lax.all_to_all(x, axis, split_axis=0, concat_axis=0, tiled=True)]
    all_to_all x1 -> x2, starting transfers between devices: 9.57 us -> 17.3 us  [swap(): return lax.all_to_all(x, axis, split_axis=0, concat_axis=0, tiled=True)]
    dot_general x3 -> x0, matrix products: 5.19 us -> none  [the longest x1 2.52 us: shards(): jnp.einsum('bd,bf->df', centered, masked, preferred_element_type=jnp.floa...]
    pallas_call x0 -> x2, Pallas kernels: none -> 5.02 us  [the longest x1 2.7 us: last_products(): pl.pallas_call(last_kernel, out_shape=(jax.ShapeDtypeStruct((features, wi...]
    unnamed x8 -> x6, local copies, waits for them, and re-layouts: 2.02 us -> 0.02 us
    all_to_all x1 -> x2, waiting for transfers between devices: 10.4 us -> 8.88 us  [swap(): return lax.all_to_all(x, axis, split_axis=0, concat_axis=0, tiled=True)]
    pad x0 -> x1, local copies, waits for them, and re-layouts: none -> 1.31 us  [shards(): extra = jnp.pad(inputs, ((0, 16 - rows), (0, half - columns)))]
  transfers between devices with their start and end apart: 1 -> 2, of which waited for: 1 -> 2; matrix products, arithmetic and copies ran while one was open for 0% -> 0% of each run, Pallas kernels for 0% -> 0%
where the time goes in v2:
time: 85.3 us; the launch traced here: 84.9 us
  blocking collectives  49.1 us (58%)
  starting transfers between devices  17.3 us (20%)
  waiting for transfers between devices  8.88 us (10%)
  Pallas kernels  5.02 us (6%)
  local copies, waits for them, and re-layouts  3.1 us (4%)
    all_to_all x3, blocking collectives, swap(): return lax.all_to_all(x, axis, split_axis=0, concat_axis=0, tiled=True)  49.1 us
    all_to_all x2, starting transfers between devices, swap(): return lax.all_to_all(x, axis, split_axis=0, concat_axis=0, tiled=True)  17.3 us
    all_to_all x2, waiting for transfers between devices, swap(): return lax.all_to_all(x, axis, split_axis=0, concat_axis=0, tiled=True)  8.88 us
    pallas_call x1, Pallas kernels, last_products(): pl.pallas_call(last_kernel, out_shape=(jax.ShapeDtypeStruct((features, wi...  2.7 us
    pallas_call x1, Pallas kernels, first_product(): pl.pallas_call(first_kernel, grid=(2,), out_shape=jax.ShapeDtypeStruct((2...  2.32 us
  transfers between devices with their start and end apart: 2, of which 2 were waited for; matrix products, arithmetic and copies ran while one was open for 0% of the time, Pallas kernels for 0%

profile of v2, /device:TPU:1, one launch (start us, length us, event | category | flops | bytes accessed | tf_op | source)
XLA Modules:
  0.0 84.9 jit_solution(14445344974358233336)
XLA Ops:
  0.6 1.3 %pad.8.extra = bf16[16,1152]{1,0:T(8,128)(2,1)} pad(bf16[4,144]{1,0:T(4,128)(2,1)} %param.4, bf16[]{:T(256)} %constant.20.clone.1), padding=0_12x0_1008 | pad | bytes 38018 | tf_op jit(solution)/shard_map/jit(_pad)/pad | solution.py:113
  1.9 2.3 %first_product.1 = bf16[2,144,1152]{2,1,0:T(8,128)(2,1)} custom-call(bf16[128,256]{1,0:T(8,128)(2,1)} %pre.3, bf16[256,2304]{1,0:T(8,128)(2,1)} %weight.3, bf16[16,1152]{1,0:T(8,128)(2,1)} %pad.8.extra), custom_call_target="tpu_custom_call" | custom-call | tf_op jit(solution)/shard_map/first_product/pallas_call | solution.py:35
  4.3 10.3 %all-to-all-start = ((bf16[2,144,1152]{2,1,0:T(8,128)(2,1)}), bf16[2,144,1152]{2,1,0:T(8,128)(2,1)S(1)}, u32[]{:S(2)}, u32[]{:S(2)}) async-start(bf16[2,144,1152]{2,1,0:T(8,128)(2,1)} %first_product.1), calls=%async_computation | async-start | bytes 1327104 | tf_op jit(solution)/shard_map/all_to_all | solution.py:13
  14.6 1.5 %all-to-all-done = bf16[2,144,1152]{2,1,0:T(8,128)(2,1)S(1)} async-done(((bf16[2,144,1152]{2,1,0:T(8,128)(2,1)}), bf16[2,144,1152]{2,1,0:T(8,128)(2,1)S(1)}, u32[]{:S(2)}, u32[]{:S(2)}) %all-to-all-start) | async-done | bytes 663584 | tf_op jit(solution)/shard_map/all_to_all | solution.py:13
  16.1 0.1 pad_maximum_fusion.1
  16.2 0.1 dynamic_update_slice.3
  16.3 0.1 slice_convert_fusion
  16.4 0.1 slice_add_fusion
  16.5 0.2 add.43
  16.7 0.0 copy-start.2
  16.7 0.2 subtract_convert_fusion
  16.9 17.5 %all_to_all.25 = bf16[32,4,1152]{2,1,0:T(4,128)(2,1)S(1)} all-to-all(bf16[32,4,1152]{2,1,0:T(4,128)(2,1)S(1)} %subtract_convert_fusion), channel_id=1, replica_groups=mesh['x'=4,'yh'=2,'core'=2,'yl'=4,'z'=8] {'x','z'}, dimensions={0} | all-to-all | bytes 589824 | tf_op jit(solution)/shard_map/all_to_all | solution.py:13
  34.4 0.1 reduce_sum.21
  34.6 0.1 concatenate.11
  34.7 0.7 broadcast_in_dim.53
  35.3 7.0 %all-to-all-start.2 = ((bf16[8,4,1440]{2,1,0:T(4,128)(2,1)}), bf16[8,4,1440]{2,1,0:T(4,128)(2,1)S(1)}, u32[]{:S(2)}, u32[]{:S(2)}) async-start(bf16[8,4,1440]{2,1,0:T(4,128)(2,1)} %broadcast_in_dim.53), calls=%async_computation.2 | async-start | bytes 196608 | tf_op jit(solution)/shard_map/all_to_all | solution.py:13
  42.3 0.0 copy-done.2
  42.3 0.1 dynamic_slice.11
  42.4 0.1 dynamic_slice.9
  42.4 7.4 %all-to-all-done.2 = bf16[8,4,1440]{2,1,0:T(4,128)(2,1)S(1)} async-done(((bf16[8,4,1440]{2,1,0:T(4,128)(2,1)}), bf16[8,4,1440]{2,1,0:T(4,128)(2,1)S(1)}, u32[]{:S(2)}, u32[]{:S(2)}) %all-to-all-start.2) | async-done | bytes 92192 | tf_op jit(solution)/shard_map/all_to_all | solution.py:13
  49.9 0.1 reshape.29
  50.1 0.2 broadcast_in_dim.54
  50.3 21.2 %all_to_all.26 = bf16[32,4,2432]{2,1,0:T(4,128)(2,1)S(1)} all-to-all(bf16[32,4,2432]{2,1,0:T(4,128)(2,1)S(1)} %broadcast_in_dim.54), channel_id=1, replica_groups=mesh['x'=4,'yh'=2,'core'=2,'yl'=4,'z'=8] {'x','z'}, dimensions={0} | all-to-all | bytes 1245184 | tf_op jit(solution)/shard_map/all_to_all | solution.py:13
  71.5 0.1 broadcast_in_dim.55
  71.7 0.1 broadcast_in_dim.56
  71.8 0.0 copy-start
  71.8 0.0 copy-start.1
  71.8 10.4 %all_to_all.27.both = bf16[2,128,2432]{2,1,0:T(8,128)(2,1)S(1)} all-to-all(bf16[2,128,2432]{2,1,0:T(8,128)(2,1)S(1)} %broadcast_in_dim.56), channel_id=1, replica_groups=mesh['x'=4,'yh'=2,'core'=2,'yl'=4,'z'=8] {'core'}, dimensions={0} | all-to-all | bytes 2490368 | tf_op jit(solution)/shard_map/all_to_all | solution.py:13
  82.2 0.0 copy-done
  82.2 0.0 copy-done.1
  82.2 2.7 %last_products.1 = (bf16[256,2304]{1,0:T(8,128)(2,1)}, bf16[2304,256]{1,0:T(8,128)(2,1)}) custom-call(bf16[2,128,2432]{2,1,0:T(8,128)(2,1)S(1)} %all_to_all.27.both, bf16[128,256]{1,0:T(8,128)(2,1)S(1)} %copy-done.1, bf16[256,2304]{1,0:T(8,128)(2,1)S(1)} %copy-done), custom_call_target="tpu_custom_call" | custom-call | tf_op jit(solution)/shard_map/last_products/pallas_call | solution.py:87
  (12 shorter events, 0.1 us)
Async XLA Ops:
  4.3 11.8 %all-to-all-start = ((bf16[2,144,1152]{2,1,0:T(8,128)(2,1)}), bf16[2,144,1152]{2,1,0:T(8,128)(2,1)S(1)}, u32[]{:S(2)}, u32[]{:S(2)}) async-start(bf16[2,144,1152]{2,1,0:T(8,128)(2,1)} %first_product.1), calls=%async_computation | async-start | bytes 1327104 | tf_op jit(solution)/shard_map/all_to_all | solution.py:13
  16.7 25.6 %copy-start.2 = (f32[2304]{0:T(1024)S(1)}, f32[2304]{0:T(1024)}, u32[]{:S(2)}) copy-start(f32[2304]{0:T(1024)} %param.5) | copy-start | bytes 27652
  35.3 14.5 %all-to-all-start.2 = ((bf16[8,4,1440]{2,1,0:T(4,128)(2,1)}), bf16[8,4,1440]{2,1,0:T(4,128)(2,1)S(1)}, u32[]{:S(2)}, u32[]{:S(2)}) async-start(bf16[8,4,1440]{2,1,0:T(4,128)(2,1)} %broadcast_in_dim.53), calls=%async_computation.2 | async-start | bytes 196608 | tf_op jit(solution)/shard_map/all_to_all | solution.py:13
  71.8 10.4 %copy-start = (bf16[256,2304]{1,0:T(8,128)(2,1)S(1)}, bf16[256,2304]{1,0:T(8,128)(2,1)}, u32[]{:S(2)}) copy-start(bf16[256,2304]{1,0:T(8,128)(2,1)} %weight.3) | copy-start | bytes 3538948
  71.8 10.4 %copy-start.1 = (bf16[128,256]{1,0:T(8,128)(2,1)S(1)}, bf16[128,256]{1,0:T(8,128)(2,1)}, u32[]{:S(2)}) copy-start(bf16[128,256]{1,0:T(8,128)(2,1)} %pre.3) | copy-start | bytes 196612

commit v3 on v2

v3 whole, which is shorter than its diff:
```python
import functools

import jax
import jax.numpy as jnp
from jax import lax
from jax.experimental import pallas as pl
from jax.experimental.pallas import tpu as pltpu
from jax.sharding import Mesh, PartitionSpec as P

BF16, F32 = jnp.bfloat16, jnp.float32
LANES, SUBLANES = 128, 8
EXTRA, CHUNKS = 16, 3
AXES = ("x", "yh", "core", "yl", "z")


def swap(x, axis):
    return lax.all_to_all(x, axis, split_axis=0, concat_axis=0, tiled=True)


def to_all(x, axis):
    return swap(jnp.broadcast_to(x[None], (lax.axis_size(axis), *x.shape)), axis)


def dot(a, b, contract):
    return lax.dot_general(a, b, ((contract[:1], contract[1:]), ((), ())), preferred_element_type=F32)


def first_kernel(pre_hbm, weight_hbm, inputs_hbm, out, pre, weight, inputs, sems):
    cores, _, half = out.shape
    batch = pre.shape[0]
    rows, columns = inputs.shape
    step = half // CHUNKS
    small = [
        pltpu.make_async_copy(pre_hbm, pre, sems.at[0]),
        pltpu.make_async_copy(inputs_hbm, inputs, sems.at[1]),
    ]
    chunks = [pl.ds(i * step, step) for i in range(cores * CHUNKS)]
    large = [
        pltpu.make_async_copy(weight_hbm.at[:, c], weight.at[:, c], sems.at[2 + i])
        for i, c in enumerate(chunks)
    ]
    for copy in small + large:
        copy.start()
    out[:, batch:, :] = jnp.zeros_like(out[:, batch:, :])
    for copy in small:
        copy.wait()
    for c in range(cores):
        out[c, batch : batch + rows, :columns] = inputs[...]
    hidden = jnp.maximum(pre[...], jnp.zeros_like(pre[...]))
    for i, c in enumerate(chunks):
        large[i].wait()
        j = i % CHUNKS
        product = dot(hidden, weight[:, c], (1, 0)).astype(BF16)
        out[i // CHUNKS, :batch, j * step : (j + 1) * step] = product


def first_product(pre, weight, inputs):
    rows = pre.shape[0]
    cores = lax.axis_size("core")
    half = weight.shape[1] // cores
    return pl.pallas_call(
        first_kernel,
        out_shape=jax.ShapeDtypeStruct((cores, rows + EXTRA, half), BF16),
        in_specs=[pl.BlockSpec(memory_space=pltpu.HBM)] * 3,
        out_specs=pl.BlockSpec(memory_space=pltpu.VMEM),
        scratch_shapes=[
            pltpu.VMEM(pre.shape, BF16),
            pltpu.VMEM(weight.shape, BF16),
            pltpu.VMEM(inputs.shape, BF16),
            pltpu.SemaphoreType.DMA((2 + cores * CHUNKS,)),
        ],
        compiler_params=pltpu.CompilerParams(vmem_limit_bytes=66_375_000),
        name="first_product",
    )(pre, weight, inputs)


def second_kernel(rows, columns, arrived, bias, out, block_out, my_bias, total):
    cores, _, half = arrived.shape
    batch = out.shape[0]
    x, yh, core, yl, z = (lax.axis_index(a) for a in AXES)
    own = yl * lax.axis_size("z") + z
    width = half * cores
    quarter = width // lax.axis_size("x")
    tile = arrived[0, batch:, :].astype(F32)
    for c in range(1, cores):
        tile += pltpu.roll(arrived[c, batch:, :].astype(F32), c * columns, 1)
    block_out[...] = tile[:, : block_out.shape[1]].astype(BF16)
    strip = pltpu.roll(tile[:SUBLANES], lax.rem(x * quarter, half) + yh * columns * cores, 1)
    strip = pltpu.roll(strip, lax.rem(own * rows, SUBLANES), 0)
    strip = jnp.where(x * quarter // half == core, strip, jnp.zeros_like(strip))
    total[...] = arrived[0, :batch, :].astype(F32) + arrived[1, :batch, :].astype(F32)
    place = pl.ds(pl.multiple_of(own * rows // SUBLANES * SUBLANES, SUBLANES), SUBLANES)
    total[place, :] -= strip
    out[...] = total[...].astype(BF16)
    whole = bias[...].reshape(1, width)
    my_bias[:, :half] = jnp.where(core == 0, whole[:, :half], whole[:, half:])
    here = pltpu.roll(whole, lax.rem(width - x * quarter, width), 1)[:, : my_bias.shape[1] - half]
    inside = lax.broadcasted_iota(jnp.int32, here.shape, 1) < quarter
    my_bias[:, half:] = jnp.where(inside, here, jnp.zeros_like(here))


def second_sum(arrived, bias, batch, rows, columns):
    _, _, half = arrived.shape
    return pl.pallas_call(
        functools.partial(second_kernel, rows, columns),
        out_shape=(
            jax.ShapeDtypeStruct((batch, half), BF16),
            jax.ShapeDtypeStruct((EXTRA, 3 * LANES), BF16),
            jax.ShapeDtypeStruct((1, half + padded_quarter(bias.shape[0])), F32),
        ),
        in_specs=[pl.BlockSpec(memory_space=pltpu.VMEM)] * 2,
        out_specs=(pl.BlockSpec(memory_space=pltpu.VMEM),) * 3,
        scratch_shapes=[pltpu.VMEM((batch, half), F32)],
        compiler_params=pltpu.CompilerParams(vmem_limit_bytes=8 << 20),
        name="second_sum",
    )(arrived, bias)


def third_kernel(arrived, block, out):
    count, rows, _ = out.shape
    half = arrived.shape[2]
    summed = arrived[...].astype(F32).sum(axis=0).astype(BF16)
    for i in range(count):
        out[i, :, :half] = summed
        out[i, :, half:] = block[:rows, :]


def third_sum(arrived, block, count):
    _, rows, half = arrived.shape
    return pl.pallas_call(
        third_kernel,
        out_shape=jax.ShapeDtypeStruct((count, rows, half + block.shape[1]), BF16),
        in_specs=[pl.BlockSpec(memory_space=pltpu.VMEM)] * 2,
        out_specs=pl.BlockSpec(memory_space=pltpu.VMEM),
        compiler_params=pltpu.CompilerParams(vmem_limit_bytes=8 << 20),
        name="third_sum",
    )(arrived, block)


def padded_quarter(width):
    return -(-(width // lax.axis_size("x")) // LANES) * LANES


def fourth_kernel(half, pair, arrived, bias, out):
    _, rows, _ = arrived.shape
    core = lax.axis_index("core")
    yhs, yls = lax.axis_size("yh"), lax.axis_size("yl")
    each = yls // lax.axis_size("core")
    padded = bias.shape[1] - half
    total = arrived[:, :, :half].astype(F32).sum(axis=0) + bias[:, :half]
    out[:, :half] = total.astype(BF16)
    for h in range(each):
        row = jnp.zeros((rows, padded), F32)
        for yh in range(yhs):
            piece = arrived[yh * yls + core * each + h, :, half:].astype(F32)
            spare = jnp.zeros((rows, padded - piece.shape[1]), F32)
            piece = jnp.concatenate([piece, spare], axis=1)
            row += pltpu.roll(piece, yh * pair, 1) if yh else piece
        place = slice(half + h * padded, half + (h + 1) * padded)
        out[:, place] = (row - bias[:, half:]).astype(BF16)


def fourth_sum(arrived, bias, half, pair):
    _, rows, _ = arrived.shape
    each = lax.axis_size("yl") // lax.axis_size("core")
    padded = bias.shape[1] - half
    return pl.pallas_call(
        functools.partial(fourth_kernel, half, pair),
        out_shape=jax.ShapeDtypeStruct((rows, half + each * padded), BF16),
        in_specs=[pl.BlockSpec(memory_space=pltpu.VMEM)] * 2,
        out_specs=pl.BlockSpec(memory_space=pltpu.VMEM),
        compiler_params=pltpu.CompilerParams(vmem_limit_bytes=8 << 20),
        name="fourth_sum",
    )(arrived, bias)


def last_kernel(both, pre, weight, decoder_out, encoder_out, decoder, encoder, sems):
    cores, rows, _ = both.shape
    features = pre.shape[1]
    half = weight.shape[1] // cores
    hidden = jnp.maximum(pre[...], jnp.zeros_like(pre[...]))
    copies = []

    def send(source, target):
        copies.append(pltpu.make_async_copy(source, target, sems.at[len(copies)]))
        copies[-1].start()

    backward = jnp.zeros((rows, features), F32)
    for c in range(cores):
        residual = both[c, :, :half]
        columns = pl.ds(c * half, half)
        decoder[c] = dot(hidden, residual, (0, 0)).astype(BF16)
        send(decoder.at[c], decoder_out.at[:, columns])
        backward += dot(residual, weight[:, columns], (1, 1))
    masked = jnp.where(pre[...] > 0, backward, jnp.zeros_like(backward)).astype(BF16)
    blocks, width = encoder.shape[:2]
    depth = rows // blocks
    padded = -(-width // LANES) * LANES
    for x in range(blocks):
        part = [
            both[c, x * depth : (x + 1) * depth, half + h * padded : half + (h + 1) * padded]
            for c in range(cores)
            for h in range(blocks // cores)
        ]
        product = dot(jnp.concatenate(part, axis=0), masked, (0, 0))
        encoder[x] = product[:width].astype(BF16)
        send(encoder.at[x], encoder_out.at[pl.ds(x * width, width), :])
    for copy in copies:
        copy.wait()


def last_products(both, pre, weight, blocks):
    cores = both.shape[0]
    features, width = weight.shape
    return pl.pallas_call(
        last_kernel,
        out_shape=(
            jax.ShapeDtypeStruct((features, width), BF16),
            jax.ShapeDtypeStruct((width, features), BF16),
        ),
        in_specs=[pl.BlockSpec(memory_space=pltpu.VMEM)] * 3,
        out_specs=(pl.BlockSpec(memory_space=pl.ANY),) * 2,
        scratch_shapes=[
            pltpu.VMEM((cores, features, width // cores), BF16),
            pltpu.VMEM((blocks, width // blocks, features), BF16),
            pltpu.SemaphoreType.DMA((cores + blocks,)),
        ],
        compiler_params=pltpu.CompilerParams(vmem_limit_bytes=16 << 20),
        name="last_products",
    )(both, pre, weight)


def shards(inputs, decoder_bias, preactivations, decoder_weight):
    rows, columns = inputs.shape
    batch = preactivations.shape[0]
    half = decoder_weight.shape[1] // lax.axis_size("core")
    pieces = lax.axis_size(("x", "z"))

    arrived = swap(first_product(preactivations, decoder_weight, inputs), "core")
    partial_sum, block, bias = second_sum(arrived, decoder_bias, batch, rows, columns)
    arrived = swap(partial_sum.reshape(pieces, rows, half), ("x", "z"))
    payload = third_sum(arrived, block, lax.axis_size(("yh", "yl")))
    arrived = swap(payload, ("yh", "yl"))
    payload = fourth_sum(arrived, bias, half, columns * lax.axis_size("core"))
    gathered = to_all(payload, ("x", "z")).reshape(batch, -1)
    both = to_all(gathered, "core")
    grad_decoder, grad_encoder = last_products(
        both, preactivations, decoder_weight, lax.axis_size("x")
    )
    return (grad_encoder, grad_decoder)


def solution(mesh):
    split = Mesh(mesh.devices.reshape(4, 2, 2, 4, 8), AXES)
    narrow, wide = ("x", "yh", "core"), ("yl", "z")
    return jax.shard_map(
        shards,
        mesh=split,
        in_specs=(P(wide, narrow), P(), P(None, narrow + wide), P(narrow + wide, None)),
        out_specs=(P(None, narrow + wide), P(narrow + wide, None)),
        check_vma=False,
    )
```

time: 85.3 us -> 82.8 us (0.971)
  blocking collectives: 49.1 us -> 75.1 us
  starting transfers between devices: 17.3 us -> 0 us
  waiting for transfers between devices: 8.88 us -> 0 us
  local copies, waits for them, and re-layouts: 3.1 us -> 0.48 us
  Pallas kernels: 5.02 us -> 6.16 us
    all_to_all x3 -> x5, blocking collectives: 49.1 us -> 75.1 us  [swap(): return lax.all_to_all(x, axis, split_axis=0, concat_axis=0, tiled=True)]
    all_to_all x2 -> x0, starting transfers between devices: 17.3 us -> none  [swap(): return lax.all_to_all(x, axis, split_axis=0, concat_axis=0, tiled=True)]
    all_to_all x2 -> x0, waiting for transfers between devices: 8.88 us -> none  [swap(): return lax.all_to_all(x, axis, split_axis=0, concat_axis=0, tiled=True)]
    pad x1 -> x0, local copies, waits for them, and re-layouts: 1.31 us -> none  [shards(): extra = jnp.pad(inputs, ((0, 16 - rows), (0, half - columns)))]
    pallas_call x1 -> x4, Pallas kernels: 2.32 us -> 3.47 us  [the longest x1 3.03 us: first_product(): pl.pallas_call(first_kernel, out_shape=jax.ShapeDtypeStruct((cores, rows...]
  transfers between devices with their start and end apart: 2 -> 0, of which waited for: 2 -> 0; matrix products, arithmetic and copies ran while one was open for 0% -> 0% of each run, Pallas kernels for 0% -> 0%
where the time goes in v3:
time: 82.8 us; the launch traced here: 82.5 us
  blocking collectives  75.1 us (91%)
  Pallas kernels  6.16 us (7%)
    all_to_all x5, blocking collectives, swap(): return lax.all_to_all(x, axis, split_axis=0, concat_axis=0, tiled=True)  75.1 us
    pallas_call x1, Pallas kernels, first_product(): pl.pallas_call(first_kernel, out_shape=jax.ShapeDtypeStruct((cores, rows...  3.03 us
    pallas_call x1, Pallas kernels, last_products(): pl.pallas_call(last_kernel, out_shape=(jax.ShapeDtypeStruct((features, wi...  2.7 us

profile of v3, /device:TPU:1, one launch (start us, length us, event | category | flops | bytes accessed | tf_op | source)
XLA Modules:
  0.0 82.5 jit_solution(4393530390697263498)
XLA Ops:
  0.6 0.0 copy-start.2
  0.6 3.0 %first_product.1 = bf16[2,144,1152]{2,1,0:T(8,128)(2,1)} custom-call(bf16[128,256]{1,0:T(8,128)(2,1)} %pre.1, bf16[256,2304]{1,0:T(8,128)(2,1)} %weight.1, bf16[4,144]{1,0:T(4,128)(2,1)} %inputs_hbm.1), custom_call_target="tpu_custom_call" | custom-call | tf_op jit(solution)/shard_map/first_product/pallas_call | solution.py:61
  3.7 11.8 %all_to_all.25.arrived = bf16[2,144,1152]{2,1,0:T(8,128)(2,1)S(1)} all-to-all(bf16[2,144,1152]{2,1,0:T(8,128)(2,1)} %first_product.1), channel_id=1, replica_groups=mesh['x'=4,'yh'=2,'core'=2,'yl'=4,'z'=8] {'core'}, dimensions={0} | all-to-all | bytes 1327104 | tf_op jit(solution)/shard_map/all_to_all | solution.py:17
  15.5 0.0 copy-done.2
  15.5 0.2 second_sum.1
  15.7 0.1 reshape.9
  15.8 17.5 %all_to_all.26.arrived = bf16[32,4,1152]{2,1,0:T(4,128)(2,1)S(1)} all-to-all(bf16[32,4,1152]{2,1,0:T(4,128)(2,1)S(1)} %reshape.9), channel_id=1, replica_groups=mesh['x'=4,'yh'=2,'core'=2,'yl'=4,'z'=8] {'x','z'}, dimensions={0} | all-to-all | bytes 589824 | tf_op jit(solution)/shard_map/all_to_all | solution.py:17
  33.3 0.1 third_sum.1
  33.5 14.2 %all_to_all.27.arrived = bf16[8,4,1536]{2,1,0:T(4,128)(2,1)S(1)} all-to-all(bf16[8,4,1536]{2,1,0:T(4,128)(2,1)S(1)} %third_sum.1), channel_id=1, replica_groups=mesh['x'=4,'yh'=2,'core'=2,'yl'=4,'z'=8] {'yh','yl'}, dimensions={0} | all-to-all | bytes 196608 | tf_op jit(solution)/shard_map/all_to_all | solution.py:17
  47.7 0.1 fourth_sum.1
  47.8 0.2 broadcast_in_dim.6
  47.9 21.2 %all_to_all.28 = bf16[32,4,2432]{2,1,0:T(4,128)(2,1)S(1)} all-to-all(bf16[32,4,2432]{2,1,0:T(4,128)(2,1)S(1)} %broadcast_in_dim.6), channel_id=1, replica_groups=mesh['x'=4,'yh'=2,'core'=2,'yl'=4,'z'=8] {'x','z'}, dimensions={0} | all-to-all | bytes 1245184 | tf_op jit(solution)/shard_map/all_to_all | solution.py:17
  69.2 0.1 broadcast_in_dim.14
  69.3 0.1 broadcast_in_dim.15
  69.4 0.0 copy-start
  69.4 0.0 copy-start.1
  69.4 10.4 %all_to_all.29.both = bf16[2,128,2432]{2,1,0:T(8,128)(2,1)S(1)} all-to-all(bf16[2,128,2432]{2,1,0:T(8,128)(2,1)S(1)} %broadcast_in_dim.15), channel_id=1, replica_groups=mesh['x'=4,'yh'=2,'core'=2,'yl'=4,'z'=8] {'core'}, dimensions={0} | all-to-all | bytes 2490368 | tf_op jit(solution)/shard_map/all_to_all | solution.py:17
  79.8 0.0 copy-done
  79.8 0.0 copy-done.1
  79.8 2.7 %last_products.1 = (bf16[256,2304]{1,0:T(8,128)(2,1)}, bf16[2304,256]{1,0:T(8,128)(2,1)}) custom-call(bf16[2,128,2432]{2,1,0:T(8,128)(2,1)S(1)} %all_to_all.29.both, bf16[128,256]{1,0:T(8,128)(2,1)S(1)} %copy-done.1, bf16[256,2304]{1,0:T(8,128)(2,1)S(1)} %copy-done), custom_call_target="tpu_custom_call" | custom-call | tf_op jit(solution)/shard_map/last_products/pallas_call | solution.py:215
Async XLA Ops:
  0.6 14.9 %copy-start.2 = (f32[2304]{0:T(1024)S(1)}, f32[2304]{0:T(1024)}, u32[]{:S(2)}) copy-start(f32[2304]{0:T(1024)} %bias.1) | copy-start | bytes 27652
  69.4 10.4 %copy-start = (bf16[256,2304]{1,0:T(8,128)(2,1)S(1)}, bf16[256,2304]{1,0:T(8,128)(2,1)}, u32[]{:S(2)}) copy-start(bf16[256,2304]{1,0:T(8,128)(2,1)} %weight.1) | copy-start | bytes 3538948
  69.4 10.4 %copy-start.1 = (bf16[128,256]{1,0:T(8,128)(2,1)S(1)}, bf16[128,256]{1,0:T(8,128)(2,1)}, u32[]{:S(2)}) copy-start(bf16[128,256]{1,0:T(8,128)(2,1)} %pre.1) | copy-start | bytes 196612

commit v4 on v1

v4 whole, which is shorter than its diff:
```python
import functools

import jax
import jax.numpy as jnp
from jax import lax
from jax.experimental import pallas as pl
from jax.experimental.pallas import tpu as pltpu
from jax.sharding import Mesh, PartitionSpec as P

BF16, F32 = jnp.bfloat16, jnp.float32
LANES, SUBLANES, CHUNKS = 128, 8, 3
AXES = ("x", "yh", "core", "ya", "yb", "za", "zb")
SIZES = (4, 2, 2, 2, 2, 4, 2)
NEAR, FAR = ("x", "yb", "zb"), ("yh", "ya", "za")
VMEM = pl.BlockSpec(memory_space=pltpu.VMEM)


def swap(x, axis):
    return lax.all_to_all(x, axis, split_axis=0, concat_axis=0, tiled=True)


def dot(a, b, contract):
    return lax.dot_general(a, b, ((contract[:1], contract[1:]), ((), ())), preferred_element_type=F32)


def small_kernel(kernel, result, limit, name, *operands):
    return pl.pallas_call(
        kernel,
        out_shape=result,
        in_specs=[VMEM] * len(operands),
        out_specs=VMEM,
        compiler_params=pltpu.CompilerParams(vmem_limit_bytes=limit << 20),
        name=name,
    )(*operands)


def row_order(batch, rows):
    shape = (batch, batch)
    new = lax.broadcasted_iota(jnp.int32, shape, 0)
    group, r = new // rows, lax.rem(new, rows)
    ya, group = lax.rem(group, 2), group // 2
    zb, group = lax.rem(group, 2), group // 2
    yb, za = lax.rem(group, 2), group // 2
    old = ((((ya * 2 + yb) * 4 + za) * 2) + zb) * rows + r
    return jnp.where(lax.broadcasted_iota(jnp.int32, shape, 1) == old, 1.0, 0.0).astype(BF16)


def first_kernel(
    pre_hbm, weight_hbm, inputs_hbm, bias_hbm, out, ordered, tile, pre, weight, inputs, bias, sems
):
    count, piece, half = out.shape
    batch, width = pre.shape[0], weight.shape[1]
    rows, columns = inputs.shape
    tiles = batch // piece
    step = half // CHUNKS
    chunks = [pl.ds(i * step, step) for i in range(width // step)]
    pairs = [(inputs_hbm, inputs), (bias_hbm, bias), (pre_hbm, pre)]
    pairs += [(weight_hbm.at[:, c], weight.at[:, c]) for c in chunks]
    copies = [pltpu.make_async_copy(a, b, sems.at[i]) for i, (a, b) in enumerate(pairs)]
    for copy in copies:
        copy.start()
    order = row_order(batch, rows)
    x, yh, core, ya, yb, za, zb = (lax.axis_index(a) for a in AXES)
    first = ((x * 2 + yh) * 2 + core) * columns
    copies[0].wait()
    copies[1].wait()
    whole = bias[...].reshape(1, width)
    here = pltpu.roll(whole, lax.rem(width - first, width), 1)[:, :columns]
    mine = inputs[...].astype(F32) - here
    spare = jnp.zeros((rows, 2 * LANES - columns), F32)
    padded = jnp.concatenate([mine, spare], axis=1)
    tile[...] = jnp.concatenate([padded[:, :LANES], padded[:, LANES:]], axis=0).astype(BF16)
    strip = jnp.concatenate([mine, jnp.zeros((rows, width - columns), F32)], axis=1)
    strip = jnp.concatenate([strip, jnp.zeros((piece - rows, width), F32)], axis=0)
    strip = pltpu.roll(pltpu.roll(strip, first, 1), ya * rows, 0)
    place = (za * 2 + yb) * 2 + zb
    copies[2].wait()
    ordered[...] = dot(order, pre[...], (1, 0)).astype(BF16)
    hidden = jnp.maximum(ordered[...], jnp.zeros_like(ordered[...]))
    for i, c in enumerate(chunks):
        copies[3 + i].wait()
        product = dot(hidden, weight[:, c], (1, 0)).reshape(tiles, piece, step)
        part = strip[:, i * step : (i + 1) * step]
        owned = lax.broadcasted_iota(jnp.int32, product.shape, 0) == place
        product = product - jnp.where(owned, part[None], jnp.zeros_like(part)[None])
        core_there, j = i // CHUNKS, i % CHUNKS
        out[core_there * tiles : (core_there + 1) * tiles, :, j * step : (j + 1) * step] = (
            product.astype(BF16)
        )


def first_product(pre, weight, inputs, bias):
    cores = lax.axis_size("core")
    near = lax.axis_size(NEAR)
    operands = (pre, weight, inputs, bias)
    return pl.pallas_call(
        first_kernel,
        out_shape=(
            pltpu.VMEM((cores * near, pre.shape[0] // near, weight.shape[1] // cores), BF16),
            pltpu.VMEM(pre.shape, BF16),
            pltpu.VMEM((SUBLANES, LANES), BF16),
        ),
        in_specs=[pl.BlockSpec(memory_space=pltpu.HBM)] * 4,
        out_specs=(VMEM,) * 3,
        scratch_shapes=[pltpu.VMEM(a.shape, a.dtype) for a in operands]
        + [pltpu.SemaphoreType.DMA((3 + cores * CHUNKS,))],
        compiler_params=pltpu.CompilerParams(vmem_limit_bytes=12 << 20),
        name="first_product",
    )(*(pltpu.with_memory_space_constraint(a, pltpu.HBM) for a in operands))


def second_kernel(arrived, tile, out):
    half = arrived.shape[2]
    summed = arrived[...].astype(F32).sum(axis=0).astype(BF16)
    for i in range(out.shape[0]):
        out[i, :, :half] = summed
        out[i, :, half:] = tile[...]


def third_kernel(half, tail, arrived, out):
    yhs, yas, zas = (lax.axis_size(a) for a in FAR)
    piece = arrived.shape[1]
    total = arrived[:, :, :half].astype(F32).sum(axis=0).astype(BF16)
    upper = lax.broadcasted_iota(jnp.int32, (piece, LANES), 0) < piece // yas
    parts, tails = [total], jnp.zeros((piece, LANES), F32)
    for za in range(zas):
        for yh in range(yhs):
            low, high = (
                arrived[(yh * yas + ya) * zas + za, :, half:].astype(F32) for ya in range(yas)
            )
            parts.append(jnp.where(upper, low, pltpu.roll(high, piece // yas, 0)).astype(BF16))
            rest = jnp.where(upper, pltpu.roll(low, piece // yas, 0), high)
            shift = (za * yhs + yh) * tail
            tails += pltpu.roll(rest, shift, 1) if shift else rest
    parts.append(tails.astype(BF16))
    payload = jnp.concatenate(parts, axis=1)
    for i in range(out.shape[0]):
        out[i] = payload


def last_kernel(tail, own, other, pre, weight, decoder_out, encoder_out, decoder, encoder, sems):
    batch, _ = own.shape
    core = lax.axis_index("core")
    cores, xs, yhs, zas = (lax.axis_size(a) for a in ("core", "x", "yh", "za"))
    half = weight.shape[1] // cores
    depth, span = batch // zas, LANES + tail
    sources = ((own, core), (other, 1 - core))
    hidden = jnp.maximum(pre[...], jnp.zeros_like(pre[...]))
    copies = []

    def send(source, target):
        copies.append(pltpu.make_async_copy(source, target, sems.at[len(copies)]))
        copies[-1].start()

    backward = jnp.zeros(pre.shape, F32)
    for k, (source, c) in enumerate(sources):
        residual = source[:, :half]
        columns = pl.ds(pl.multiple_of(c * half, LANES), half)
        decoder[k] = dot(hidden, residual, (0, 0)).astype(BF16)
        send(decoder.at[k], decoder_out.at[:, columns])
        backward += dot(residual, weight[:, columns], (1, 1))
    masked = jnp.where(pre[...] > 0, backward, jnp.zeros_like(backward)).astype(BF16)

    lane = lax.broadcasted_iota(jnp.int32, (depth, LANES), 1) // (yhs * tail)
    ends = []
    for source, _ in sources:
        pieces = [
            source[x * depth : (x + 1) * depth, half + zas * yhs * LANES :].astype(F32)
            for x in range(xs)
        ]
        blocks = []
        for za in range(zas):
            block = jnp.zeros((depth, LANES), F32)
            for x in range(xs):
                shift = (x - za) * yhs * tail % LANES
                moved = pltpu.roll(pieces[x], shift, 1) if shift else pieces[x]
                block = jnp.where(lane == x, moved, block)
            blocks.append(block.astype(BF16))
        ends.append(dot(jnp.concatenate(blocks, axis=0), masked, (0, 0)).astype(BF16))

    for x in range(xs):
        for k, (source, c) in enumerate(sources):
            size = yhs * LANES
            part = [
                source[x * depth : (x + 1) * depth, half + za * size : half + (za + 1) * size]
                for za in range(zas)
            ]
            product = dot(jnp.concatenate(part, axis=0), masked, (0, 0)).astype(BF16)
            for yh in range(yhs):
                start = pl.multiple_of(((x * yhs + yh) * cores + c) * span, tail)
                encoder[pl.ds(start, LANES), :] = product[yh * LANES : (yh + 1) * LANES]
                end = (x * yhs + yh) * tail
                encoder[pl.ds(pl.multiple_of(start + LANES, tail), tail), :] = ends[k][end : end + tail]
        block = pl.ds(x * yhs * cores * span, yhs * cores * span)
        send(encoder.at[block], encoder_out.at[block])
    for copy in copies:
        copy.wait()


def last_products(own, other, pre, weight, tail):
    cores = lax.axis_size("core")
    features, width = weight.shape
    return pl.pallas_call(
        functools.partial(last_kernel, tail),
        out_shape=(
            jax.ShapeDtypeStruct((features, width), BF16),
            jax.ShapeDtypeStruct((width, features), BF16),
        ),
        in_specs=[VMEM] * 4,
        out_specs=(pl.BlockSpec(memory_space=pl.ANY),) * 2,
        scratch_shapes=[
            pltpu.VMEM((cores, features, width // cores), BF16),
            pltpu.VMEM((width, features), BF16),
            pltpu.SemaphoreType.DMA((cores + lax.axis_size("x"),)),
        ],
        compiler_params=pltpu.CompilerParams(vmem_limit_bytes=20 << 20),
        name="last_products",
    )(own, other, pre, weight)


def shards(inputs, decoder_bias, preactivations, decoder_weight):
    columns = inputs.shape[1]
    batch, width = preactivations.shape[0], decoder_weight.shape[1]
    half = width // lax.axis_size("core")
    tail = columns - LANES
    near, far = lax.axis_size(NEAR), lax.axis_size(FAR)
    piece = batch // near

    pieces, ordered, tile = first_product(preactivations, decoder_weight, inputs, decoder_bias)
    arrived = swap(pieces, ("core", *NEAR))
    shape = jax.ShapeDtypeStruct((far, piece, half + LANES), BF16)
    arrived = swap(small_kernel(second_kernel, shape, 8, "second_sum", arrived, tile), FAR)
    shape = jax.ShapeDtypeStruct((near, piece, width), BF16)
    kernel = functools.partial(third_kernel, half, tail)
    own = swap(small_kernel(kernel, shape, 8, "third_sum", arrived), NEAR).reshape(batch, width)
    other = lax.ppermute(own, "core", [(0, 1), (1, 0)])
    grad_decoder, grad_encoder = last_products(own, other, ordered, decoder_weight, tail)
    return (grad_encoder, grad_decoder)


def solution(mesh):
    split = Mesh(mesh.devices.reshape(SIZES), AXES)
    narrow, wide = AXES[:3], AXES[3:]
    return jax.shard_map(
        shards,
        mesh=split,
        in_specs=(P(wide, narrow), P(), P(None, narrow + wide), P(narrow + wide, None)),
        out_specs=(P(None, narrow + wide), P(narrow + wide, None)),
        check_vma=False,
    )
```

time: 90.1 us -> 74.8 us (0.83)
  waiting for transfers between devices: 10.4 us -> 1.61 us
  starting transfers between devices: 9.57 us -> 4 us
  matrix products: 5.19 us -> 0 us
  Pallas kernels: 0 us -> 5.07 us
  blocking collectives: 59.6 us -> 63.2 us
  local copies, waits for them, and re-layouts: 2.99 us -> 0.01 us
  other arithmetic: 1.12 us -> 0 us
    all_to_all x1 -> x0, waiting for transfers between devices: 10.4 us -> none  [swap(): return lax.all_to_all(x, axis, split_axis=0, concat_axis=0, tiled=True)]
    all_to_all x1 -> x0, starting transfers between devices: 9.57 us -> none  [swap(): return lax.all_to_all(x, axis, split_axis=0, concat_axis=0, tiled=True)]
    dot_general x3 -> x0, matrix products: 5.19 us -> none  [the longest x1 2.52 us: shards(): jnp.einsum('bd,bf->df', centered, masked, preferred_element_type=jnp.floa...]
    pallas_call x0 -> x4, Pallas kernels: none -> 5.07 us  [the longest x1 2.6 us: last_products(): pl.pallas_call(functools.partial(last_kernel, tail), out_shape=(jax.Shape...]
    ppermute x0 -> x1, starting transfers between devices: none -> 4 us  [shards(): other = lax.ppermute(own, 'core', [(0, 1), (1, 0)])]
    all_to_all x3, blocking collectives: 59.6 us -> 63.2 us  [swap(): return lax.all_to_all(x, axis, split_axis=0, concat_axis=0, tiled=True)]
    unnamed x8 -> x2, local copies, waits for them, and re-layouts: 2.02 us -> 0.01 us
    ppermute x0 -> x1, waiting for transfers between devices: none -> 1.61 us  [shards(): other = lax.ppermute(own, 'core', [(0, 1), (1, 0)])]
where the time goes in v4:
time: 74.8 us; the launch traced here: 74.5 us
  blocking collectives  63.2 us (84%)
  Pallas kernels  5.07 us (7%)
  starting transfers between devices  4 us (5%)
  waiting for transfers between devices  1.61 us (2%)
    all_to_all x3, blocking collectives, swap(): return lax.all_to_all(x, axis, split_axis=0, concat_axis=0, tiled=True)  63.2 us
    ppermute x1, starting transfers between devices, shards(): other = lax.ppermute(own, 'core', [(0, 1), (1, 0)])  4 us
    pallas_call x1, Pallas kernels, last_products(): pl.pallas_call(functools.partial(last_kernel, tail), out_shape=(jax.Shape...  2.6 us
    pallas_call x1, Pallas kernels, first_product(): pl.pallas_call(first_kernel, out_shape=(pltpu.VMEM((cores * near, pre.sha...  2.28 us
    ppermute x1, waiting for transfers between devices, shards(): other = lax.ppermute(own, 'core', [(0, 1), (1, 0)])  1.61 us
  transfers between devices with their start and end apart: 1, of which 1 were waited for; matrix products, arithmetic and copies ran while one was open for 0% of the time, Pallas kernels for 0%

profile of v4, /device:TPU:1, one launch (start us, length us, event | category | flops | bytes accessed | tf_op | source)
XLA Modules:
  0.0 74.5 jit_solution(12993133661018293992)
XLA Ops:
  0.6 2.3 %first_product.1 = (bf16[32,8,1152]{2,1,0:T(8,128)(2,1)S(1)}, bf16[128,256]{1,0:T(8,128)(2,1)S(1)}, bf16[8,128]{1,0:T(8,128)(2,1)S(1)}) custom-call(bf16[128,256]{1,0:T(8,128)(2,1)} %pre_hbm.1, bf16[256,2304]{1,0:T(8,128)(2,1)} %weight.1, bf16[4,144]{1,0:T(4,128)(2,1)} %inputs_hbm.1, f32[2304]{0:T(1024)} %bias_hbm.1), custom_call_target="tpu_custom_call" | custom-call | tf_op jit(solution)/shard_map/first_product/pallas_call | solution.py:96
  2.9 21.2 %all_to_all.15.arrived = bf16[32,8,1152]{2,1,0:T(8,128)(2,1)S(1)} all-to-all(bf16[32,8,1152]{2,1,0:T(8,128)(2,1)S(1)} %get-tuple-element.7), channel_id=1, replica_groups=mesh['x'=4,'yh'=2,'core'=2,'ya'=2,'yb'=2,'za'=4,'zb'=2] {'core','x','yb'..., dimensions={0} | all-to-all | bytes 1179648 | tf_op jit(solution)/shard_map/all_to_all | solution.py:19
  24.1 0.1 second_sum.1
  24.2 25.5 %all_to_all.16.arrived = bf16[16,8,1280]{2,1,0:T(8,128)(2,1)S(1)} all-to-all(bf16[16,8,1280]{2,1,0:T(8,128)(2,1)S(1)} %second_sum.1), channel_id=1, replica_groups=mesh['x'=4,'yh'=2,'core'=2,'ya'=2,'yb'=2,'za'=4,'zb'=2] {'yh','ya','za'}, dimensions={0} | all-to-all | bytes 655360 | tf_op jit(solution)/shard_map/all_to_all | solution.py:19
  49.7 0.0 copy-start
  49.7 0.1 third_sum.1
  49.8 16.5 %all_to_all.17 = bf16[16,8,2304]{2,1,0:T(8,128)(2,1)S(1)} all-to-all(bf16[16,8,2304]{2,1,0:T(8,128)(2,1)S(1)} %third_sum.1), channel_id=1, replica_groups=mesh['x'=4,'yh'=2,'core'=2,'ya'=2,'yb'=2,'za'=4,'zb'=2] {'x','yb','zb'}, dimensions={0} | all-to-all | bytes 1179648 | tf_op jit(solution)/shard_map/all_to_all | solution.py:19
  66.3 4.0 %collective-permute-start = (bf16[128,2304]{1,0:T(8,128)(2,1)S(1)}, bf16[128,2304]{1,0:T(8,128)(2,1)S(1)}, u32[]{:S(2)}, u32[]{:S(2)}) collective-permute-start(bf16[128,2304]{1,0:T(8,128)(2,1)S(1)} %bitcast.1), channel_id=1, source_target_pairs={{0,32},{32,0},{1,33},{33,1},{2,34},{34,2},{3,35},{35,3},{4,36},{36... | collective-permute-start | bytes 1769480 | tf_op jit(solution)/shard_map/ppermute | solution.py:236
  70.3 1.6 %collective-permute-done.other = bf16[128,2304]{1,0:T(8,128)(2,1)S(1)} collective-permute-done((bf16[128,2304]{1,0:T(8,128)(2,1)S(1)}, bf16[128,2304]{1,0:T(8,128)(2,1)S(1)}, u32[]{:S(2)}, u32[]{:S(2)}) %collective-permute-start) | collective-permute-done | bytes 589856 | tf_op jit(solution)/shard_map/ppermute | solution.py:236
  71.9 0.0 copy-done
  71.9 2.6 %last_products.1 = (bf16[256,2304]{1,0:T(8,128)(2,1)}, bf16[2304,256]{1,0:T(8,128)(2,1)}) custom-call(bf16[128,2304]{1,0:T(8,128)(2,1)S(1)} %bitcast.2, bf16[128,2304]{1,0:T(8,128)(2,1)S(1)} %collective-permute-done.other, bf16[128,256]{1,0:T(8,128)(2,1)S(1)} %get-tuple-element.9.pre, bf16[256,2304]{1,0:T(8,128)(2,1)S(1)} %copy-done), custom_call_target="tpu_custom_call" | custom-call | tf_op jit(solution)/shard_map/last_products/pallas_call | solution.py:203
Async XLA Ops:
  49.7 22.2 %copy-start = (bf16[256,2304]{1,0:T(8,128)(2,1)S(1)}, bf16[256,2304]{1,0:T(8,128)(2,1)}, u32[]{:S(2)}) copy-start(bf16[256,2304]{1,0:T(8,128)(2,1)} %weight.1) | copy-start | bytes 3538948
  66.3 5.6 %collective-permute-start = (bf16[128,2304]{1,0:T(8,128)(2,1)S(1)}, bf16[128,2304]{1,0:T(8,128)(2,1)S(1)}, u32[]{:S(2)}, u32[]{:S(2)}) collective-permute-start(bf16[128,2304]{1,0:T(8,128)(2,1)S(1)} %bitcast.1), channel_id=1, source_target_pairs={{0,32},{32,0},{1,33},{33,1},{2,34},{34,2},{3,35},{35,3},{4,36},{36... | collective-permute-start | bytes 1769480 | tf_op jit(solution)/shard_map/ppermute | solution.py:236

commit v5 on v4

--- a/solution.py
+++ b/solution.py
@@ -46,21 +46,22 @@
 
 
 def first_kernel(
-    pre_hbm, weight_hbm, inputs_hbm, bias_hbm, out, ordered, tile, pre, weight, inputs, bias, sems
+    pre_hbm, weight_hbm, inputs_hbm, bias_hbm, out, ordered, tile, strip, pre, weight, inputs, bias, sems
 ):
-    count, piece, half = out.shape
-    batch, width = pre.shape[0], weight.shape[1]
+    batch, half = out.shape
+    piece, width = strip.shape[0], bias.shape[0]
     rows, columns = inputs.shape
-    tiles = batch // piece
     step = half // CHUNKS
-    chunks = [pl.ds(i * step, step) for i in range(width // step)]
+    x, yh, core, ya, yb, za, zb = (lax.axis_index(a) for a in AXES)
+    there = (1 - core) * half
     pairs = [(inputs_hbm, inputs), (bias_hbm, bias), (pre_hbm, pre)]
-    pairs += [(weight_hbm.at[:, c], weight.at[:, c]) for c in chunks]
+    for i in range(CHUNKS):
+        columns_there = pl.ds(pl.multiple_of(there + i * step, LANES), step)
+        pairs.append((weight_hbm.at[:, columns_there], weight.at[:, pl.ds(i * step, step)]))
     copies = [pltpu.make_async_copy(a, b, sems.at[i]) for i, (a, b) in enumerate(pairs)]
     for copy in copies:
         copy.start()
     order = row_order(batch, rows)
-    x, yh, core, ya, yb, za, zb = (lax.axis_index(a) for a in AXES)
     first = ((x * 2 + yh) * 2 + core) * columns
     copies[0].wait()
     copies[1].wait()
@@ -70,43 +71,94 @@
     spare = jnp.zeros((rows, 2 * LANES - columns), F32)
     padded = jnp.concatenate([mine, spare], axis=1)
     tile[...] = jnp.concatenate([padded[:, :LANES], padded[:, LANES:]], axis=0).astype(BF16)
-    strip = jnp.concatenate([mine, jnp.zeros((rows, width - columns), F32)], axis=1)
-    strip = jnp.concatenate([strip, jnp.zeros((piece - rows, width), F32)], axis=0)
-    strip = pltpu.roll(pltpu.roll(strip, first, 1), ya * rows, 0)
-    place = (za * 2 + yb) * 2 + zb
+    line = jnp.concatenate([mine, jnp.zeros((rows, half - columns), F32)], axis=1)
+    line = jnp.concatenate([line, jnp.zeros((piece - rows, half), F32)], axis=0)
+    strip[...] = pltpu.roll(pltpu.roll(line, lax.rem(first, half), 1), ya * rows, 0)
     copies[2].wait()
     ordered[...] = dot(order, pre[...], (1, 0)).astype(BF16)
     hidden = jnp.maximum(ordered[...], jnp.zeros_like(ordered[...]))
-    for i, c in enumerate(chunks):
+    place = jnp.where(first // half == core, batch, (za * 2 + yb) * 2 + zb)
+    for i in range(CHUNKS):
         copies[3 + i].wait()
-        product = dot(hidden, weight[:, c], (1, 0)).reshape(tiles, piece, step)
-        part = strip[:, i * step : (i + 1) * step]
-        owned = lax.broadcasted_iota(jnp.int32, product.shape, 0) == place
-        product = product - jnp.where(owned, part[None], jnp.zeros_like(part)[None])
-        core_there, j = i // CHUNKS, i % CHUNKS
-        out[core_there * tiles : (core_there + 1) * tiles, :, j * step : (j + 1) * step] = (
-            product.astype(BF16)
-        )
+        part = pl.ds(i * step, step)
+        product = dot(hidden, weight[:, part], (1, 0))
+        out[:, part] = less(product, strip[:, part], place).astype(BF16)
+
+
+def less(product, strip, place):
+    piece = strip.shape[0]
+    pieces = product.reshape(product.shape[0] // piece, *strip.shape)
+    owned = lax.broadcasted_iota(jnp.int32, pieces.shape, 0) == place
+    pieces = pieces - jnp.where(owned, strip[None], jnp.zeros_like(strip)[None])
+    return pieces.reshape(product.shape)
 
 
 def first_product(pre, weight, inputs, bias):
-    cores = lax.axis_size("core")
-    near = lax.axis_size(NEAR)
+    half = weight.shape[1] // lax.axis_size("core")
     operands = (pre, weight, inputs, bias)
     return pl.pallas_call(
         first_kernel,
         out_shape=(
-            pltpu.VMEM((cores * near, pre.shape[0] // near, weight.shape[1] // cores), BF16),
+            pltpu.VMEM((pre.shape[0], half), BF16),
             pltpu.VMEM(pre.shape, BF16),
             pltpu.VMEM((SUBLANES, LANES), BF16),
+            pltpu.VMEM((SUBLANES, half), F32),
         ),
         in_specs=[pl.BlockSpec(memory_space=pltpu.HBM)] * 4,
-        out_specs=(VMEM,) * 3,
-        scratch_shapes=[pltpu.VMEM(a.shape, a.dtype) for a in operands]
-        + [pltpu.SemaphoreType.DMA((3 + cores * CHUNKS,))],
+        out_specs=(VMEM,) * 4,
+        scratch_shapes=[
+            pltpu.VMEM(pre.shape, BF16),
+            pltpu.VMEM((weight.shape[0], half), BF16),
+            pltpu.VMEM(inputs.shape, BF16),
+            pltpu.VMEM(bias.shape, F32),
+            pltpu.SemaphoreType.DMA((3 + CHUNKS,)),
+        ],
         compiler_params=pltpu.CompilerParams(vmem_limit_bytes=12 << 20),
         name="first_product",
     )(*(pltpu.with_memory_space_constraint(a, pltpu.HBM) for a in operands))
+
+
+def own_kernel(ordered, strip, weight_hbm, out, weight, sems):
+    batch, half = out.shape
+    step = half // CHUNKS
+    x, yh, core, ya, yb, za, zb = (lax.axis_index(a) for a in AXES)
+    copies = []
+    for i in range(CHUNKS):
+        columns = pl.ds(pl.multiple_of(core * half + i * step, LANES), step)
+        target = weight.at[:, pl.ds(i * step, step)]
+        copies.append(pltpu.make_async_copy(weight_hbm.at[:, columns], target, sems.at[i]))
+        copies[-1].start()
+    hidden = jnp.maximum(ordered[...], jnp.zeros_like(ordered[...]))
+    place = jnp.where(x * 2 // lax.axis_size("x") == core, (za * 2 + yb) * 2 + zb, batch)
+    for i in range(CHUNKS):
+        copies[i].wait()
+        part = pl.ds(i * step, step)
+        product = dot(hidden, weight[:, part], (1, 0))
+        out[:, part] = less(product, strip[:, part], place)
+
+
+def own_product(ordered, strip, weight):
+    batch, features = ordered.shape
+    half = strip.shape[1]
+    return pl.pallas_call(
+        own_kernel,
+        out_shape=pltpu.VMEM((batch, half), F32),
+        in_specs=[VMEM, VMEM, pl.BlockSpec(memory_space=pltpu.HBM)],
+        out_specs=VMEM,
+        scratch_shapes=[
+            pltpu.VMEM((features, half), BF16),
+            pltpu.SemaphoreType.DMA((CHUNKS,)),
+        ],
+        compiler_params=pltpu.CompilerParams(vmem_limit_bytes=8 << 20),
+        cost_estimate=pl.CostEstimate(
+            flops=2 * batch * features * half, bytes_accessed=features * half * 2, transcendentals=0
+        ),
+        name="own_product",
+    )(ordered, strip, pltpu.with_memory_space_constraint(weight, pltpu.HBM))
+
+
+def join_kernel(own, arrived, out):
+    out[...] = (own[...] + arrived[...].astype(F32)).reshape(out.shape).astype(BF16)
 
 
 def second_kernel(arrived, tile, out):
@@ -138,28 +190,58 @@
         out[i] = payload
 
 
-def last_kernel(tail, own, other, pre, weight, decoder_out, encoder_out, decoder, encoder, sems):
-    batch, _ = own.shape
+def near_kernel(own, pre, weight, decoder_out, backward, decoder, sem):
+    half = decoder.shape[1]
+    core = lax.axis_index("core")
+    hidden = jnp.maximum(pre[...], jnp.zeros_like(pre[...]))
+    columns = pl.ds(pl.multiple_of(core * half, LANES), half)
+    decoder[...] = dot(hidden, own[:, :half], (0, 0)).astype(BF16)
+    copy = pltpu.make_async_copy(decoder, decoder_out.at[:, columns], sem)
+    copy.start()
+    backward[...] = dot(own[:, :half], weight[:, columns], (1, 1))
+    copy.wait()
+
+
+def near_products(own, pre, weight):
+    features, width = weight.shape
+    half = width // lax.axis_size("core")
+    return pl.pallas_call(
+        near_kernel,
+        out_shape=(pltpu.HBM((features, width), BF16), pltpu.VMEM(pre.shape, F32)),
+        in_specs=[VMEM] * 3,
+        out_specs=(pl.BlockSpec(memory_space=pltpu.HBM), VMEM),
+        scratch_shapes=[pltpu.VMEM((features, half), BF16), pltpu.SemaphoreType.DMA],
+        compiler_params=pltpu.CompilerParams(vmem_limit_bytes=10 << 20),
+        cost_estimate=pl.CostEstimate(
+            flops=4 * pre.shape[0] * features * half,
+            bytes_accessed=features * width * 2,
+            transcendentals=0,
+        ),
+        name="near_products",
+    )(own, pre, weight)
+
+
+def last_kernel(
+    tail, own, other, pre, weight, backward, _, decoder_out, encoder_out, decoder, encoder, sems
+):
+    batch, half = other.shape[0], decoder.shape[1]
     core = lax.axis_index("core")
     cores, xs, yhs, zas = (lax.axis_size(a) for a in ("core", "x", "yh", "za"))
-    half = weight.shape[1] // cores
     depth, span = batch // zas, LANES + tail
     sources = ((own, core), (other, 1 - core))
-    hidden = jnp.maximum(pre[...], jnp.zeros_like(pre[...]))
     copies = []
 
     def send(source, target):
         copies.append(pltpu.make_async_copy(source, target, sems.at[len(copies)]))
         copies[-1].start()
 
-    backward = jnp.zeros(pre.shape, F32)
-    for k, (source, c) in enumerate(sources):
-        residual = source[:, :half]
-        columns = pl.ds(pl.multiple_of(c * half, LANES), half)
-        decoder[k] = dot(hidden, residual, (0, 0)).astype(BF16)
-        send(decoder.at[k], decoder_out.at[:, columns])
-        backward += dot(residual, weight[:, columns], (1, 1))
-    masked = jnp.where(pre[...] > 0, backward, jnp.zeros_like(backward)).astype(BF16)
+    columns = pl.ds(pl.multiple_of((1 - core) * half, LANES), half)
+    residual = other[:, :half]
+    total = backward[...] + dot(residual, weight[:, columns], (1, 1))
+    masked = jnp.where(pre[...] > 0, total, jnp.zeros_like(total)).astype(BF16)
+    hidden = jnp.maximum(pre[...], jnp.zeros_like(pre[...]))
+    decoder[...] = dot(hidden, residual, (0, 0)).astype(BF16)
+    send(decoder, decoder_out.at[:, columns])
 
     lane = lax.broadcasted_iota(jnp.int32, (depth, LANES), 1) // (yhs * tail)
     ends = []
@@ -197,25 +279,26 @@
         copy.wait()
 
 
-def last_products(own, other, pre, weight, tail):
-    cores = lax.axis_size("core")
+def last_products(own, other, pre, weight, backward, decoder, tail):
     features, width = weight.shape
+    raw = pl.BlockSpec(memory_space=pltpu.HBM)
     return pl.pallas_call(
         functools.partial(last_kernel, tail),
         out_shape=(
             jax.ShapeDtypeStruct((features, width), BF16),
             jax.ShapeDtypeStruct((width, features), BF16),
         ),
-        in_specs=[VMEM] * 4,
-        out_specs=(pl.BlockSpec(memory_space=pl.ANY),) * 2,
+        in_specs=[VMEM] * 5 + [raw],
+        out_specs=(raw, raw),
         scratch_shapes=[
-            pltpu.VMEM((cores, features, width // cores), BF16),
+            pltpu.VMEM((features, width // lax.axis_size("core")), BF16),
             pltpu.VMEM((width, features), BF16),
-            pltpu.SemaphoreType.DMA((cores + lax.axis_size("x"),)),
+            pltpu.SemaphoreType.DMA((1 + lax.axis_size("x"),)),
         ],
+        input_output_aliases={5: 0},
         compiler_params=pltpu.CompilerParams(vmem_limit_bytes=20 << 20),
         name="last_products",
-    )(own, other, pre, weight)
+    )(own, other, pre, weight, backward, decoder)
 
 
 def shards(inputs, decoder_bias, preactivations, decoder_weight):
@@ -225,16 +308,25 @@
     tail = columns - LANES
     near, far = lax.axis_size(NEAR), lax.axis_size(FAR)
     piece = batch // near
-
-    pieces, ordered, tile = first_product(preactivations, decoder_weight, inputs, decoder_bias)
-    arrived = swap(pieces, ("core", *NEAR))
+    partner = [(0, 1), (1, 0)]
+
+    theirs, ordered, tile, strip = first_product(
+        preactivations, decoder_weight, inputs, decoder_bias
+    )
+    arrived = lax.ppermute(theirs, "core", partner)
+    mine = own_product(ordered, strip, decoder_weight)
+    shape = jax.ShapeDtypeStruct((near, piece, half), BF16)
+    arrived = swap(small_kernel(join_kernel, shape, 8, "join_cores", mine, arrived), NEAR)
     shape = jax.ShapeDtypeStruct((far, piece, half + LANES), BF16)
     arrived = swap(small_kernel(second_kernel, shape, 8, "second_sum", arrived, tile), FAR)
     shape = jax.ShapeDtypeStruct((near, piece, width), BF16)
     kernel = functools.partial(third_kernel, half, tail)
     own = swap(small_kernel(kernel, shape, 8, "third_sum", arrived), NEAR).reshape(batch, width)
-    other = lax.ppermute(own, "core", [(0, 1), (1, 0)])
-    grad_decoder, grad_encoder = last_products(own, other, ordered, decoder_weight, tail)
+    other = lax.ppermute(own, "core", partner)
+    decoder, backward = near_products(own, ordered, decoder_weight)
+    grad_decoder, grad_encoder = last_products(
+        own, other, ordered, decoder_weight, backward, decoder, tail
+    )
     return (grad_encoder, grad_decoder)
 
 

time: 74.8 us -> 73.2 us (0.979)
  blocking collectives: 63.2 us -> 52.6 us
  starting transfers between devices: 4 us -> 12.7 us
  Pallas kernels: 5.07 us -> 6.55 us
  waiting for transfers between devices: 1.61 us -> 0.35 us
    all_to_all x3, blocking collectives: 63.2 us -> 52.6 us  [swap(): return lax.all_to_all(x, axis, split_axis=0, concat_axis=0, tiled=True)]
    ppermute x1 -> x2, starting transfers between devices: 4 us -> 12.7 us  [the longest x1 8.75 us: shards(): arrived = lax.ppermute(theirs, 'core', partner)]
    pallas_call x1 -> x3, Pallas kernels: 2.28 us -> 4.48 us  [the longest x1 1.69 us: first_product(): pl.pallas_call(first_kernel, out_shape=(pltpu.VMEM((pre.shape[0], half),...]
    ppermute x1 -> x2, waiting for transfers between devices: 1.61 us -> 0.35 us  [the longest x1 0.34 us: shards(): other = lax.ppermute(own, 'core', partner)]
  transfers between devices with their start and end apart: 1 -> 2, of which waited for: 1 -> 1; matrix products, arithmetic and copies ran while one was open for 0% -> 0% of each run, Pallas kernels for 0% -> 4%
where the time goes in v5:
time: 73.2 us; the launch traced here: 72.9 us
  blocking collectives  52.6 us (72%)
  starting transfers between devices  12.7 us (17%)
  Pallas kernels  6.55 us (9%)
    all_to_all x3, blocking collectives, swap(): return lax.all_to_all(x, axis, split_axis=0, concat_axis=0, tiled=True)  52.6 us
    ppermute x1, starting transfers between devices, shards(): arrived = lax.ppermute(theirs, 'core', partner)  8.75 us
    ppermute x1, starting transfers between devices, shards(): other = lax.ppermute(own, 'core', partner)  3.94 us
    pallas_call x1, Pallas kernels, last_products(): pl.pallas_call(functools.partial(last_kernel, tail), out_shape=(jax.Shape...  1.87 us
    pallas_call x1, Pallas kernels, first_product(): pl.pallas_call(first_kernel, out_shape=(pltpu.VMEM((pre.shape[0], half),...  1.69 us
    pallas_call x1, Pallas kernels, own_product(): pl.pallas_call(own_kernel, out_shape=pltpu.VMEM((batch, half), F32), in_s...  1.54 us
  transfers between devices with their start and end apart: 2, of which 1 were waited for; matrix products, arithmetic and copies ran while one was open for 0% of the time, Pallas kernels for 4%

profile of v5, /device:TPU:1, one launch (start us, length us, event | category | flops | bytes accessed | tf_op | source)
XLA Modules:
  0.0 72.9 jit_solution(4093475844720567585)
XLA Ops:
  0.6 1.7 %first_product.1 = (bf16[128,1152]{1,0:T(8,128)(2,1)S(1)}, bf16[128,256]{1,0:T(8,128)(2,1)S(1)}, bf16[8,128]{1,0:T(8,128)(2,1)S(1)}, f32[8,1152]{1,0:T(8,128)S(1)}) custom-call(bf16[128,256]{1,0:T(8,128)(2,1)} %pre_hbm.1, bf16[256,2304]{1,0:T(8,128)(2,1)} %weight.3, bf16[4,144]{1,0:T(4,128)(2,1)} %inputs_hbm.1, f32[2304]{0:T(1024)} %bias_hbm.1), custom_call_target="tpu_custom_call" | custom-call | tf_op jit(solution)/shard_map/first_product/pallas_call | solution.py:99
  2.3 8.7 %collective-permute-start = (bf16[128,1152]{1,0:T(8,128)(2,1)S(1)}, bf16[128,1152]{1,0:T(8,128)(2,1)S(1)}, u32[]{:S(2)}, u32[]{:S(2)}) collective-permute-start(bf16[128,1152]{1,0:T(8,128)(2,1)S(1)} %get-tuple-element.12), channel_id=1, source_target_pairs={{0,32},{32,0},{1,33},{33,1},{2,34},{34,2},{3,35},{35,3},{4,36},{36... | collective-permute-start | bytes 884744 | tf_op jit(solution)/shard_map/ppermute | solution.py:316
  11.1 1.5 %own_product.1.own = f32[128,1152]{1,0:T(8,128)S(1)} custom-call(bf16[128,256]{1,0:T(8,128)(2,1)S(1)} %get-tuple-element.10.ordered.pre, f32[8,1152]{1,0:T(8,128)S(1)} %get-tuple-element.11.strip, bf16[256,2304]{1,0:T(8,128)(2,1)} %weight.3), custom_call_target="tpu_custom_call" | custom-call | flops 75497472 | bytes 589824 | tf_op jit(solution)/shard_map/own_product/pallas_call | solution.py:143
  12.6 0.0 collective-permute-done.arrived
  12.6 0.1 join_cores.1
  12.7 10.2 %all_to_all.15.arrived = bf16[16,8,1152]{2,1,0:T(8,128)(2,1)S(1)} all-to-all(bf16[16,8,1152]{2,1,0:T(8,128)(2,1)S(1)} %join_cores.1), channel_id=1, replica_groups=mesh['x'=4,'yh'=2,'core'=2,'ya'=2,'yb'=2,'za'=4,'zb'=2] {'x','yb','zb'}, dimensions={0} | all-to-all | bytes 589824 | tf_op jit(solution)/shard_map/all_to_all | solution.py:19
  22.9 0.1 second_sum.1
  23.0 24.5 %all_to_all.16.arrived = bf16[16,8,1280]{2,1,0:T(8,128)(2,1)S(1)} all-to-all(bf16[16,8,1280]{2,1,0:T(8,128)(2,1)S(1)} %second_sum.1), channel_id=1, replica_groups=mesh['x'=4,'yh'=2,'core'=2,'ya'=2,'yb'=2,'za'=4,'zb'=2] {'yh','ya','za'}, dimensions={0} | all-to-all | bytes 655360 | tf_op jit(solution)/shard_map/all_to_all | solution.py:19
  47.5 0.0 copy-start
  47.5 0.1 third_sum.1
  47.6 17.9 %all_to_all.17 = bf16[16,8,2304]{2,1,0:T(8,128)(2,1)S(1)} all-to-all(bf16[16,8,2304]{2,1,0:T(8,128)(2,1)S(1)} %third_sum.1), channel_id=1, replica_groups=mesh['x'=4,'yh'=2,'core'=2,'ya'=2,'yb'=2,'za'=4,'zb'=2] {'x','yb','zb'}, dimensions={0} | all-to-all | bytes 1179648 | tf_op jit(solution)/shard_map/all_to_all | solution.py:19
  65.5 3.9 %collective-permute-start.1 = (bf16[128,2304]{1,0:T(8,128)(2,1)S(1)}, bf16[128,2304]{1,0:T(8,128)(2,1)S(1)}, u32[]{:S(2)}, u32[]{:S(2)}) collective-permute-start(bf16[128,2304]{1,0:T(8,128)(2,1)S(1)} %bitcast.1), channel_id=1, source_target_pairs={{0,32},{32,0},{1,33},{33,1},{2,34},{34,2},{3,35},{35,3},{4,36},{36... | collective-permute-start | bytes 1769480 | tf_op jit(solution)/shard_map/ppermute | solution.py:325
  69.4 0.0 copy-done
  69.4 1.2 %near_products.1 = (bf16[256,2304]{1,0:T(8,128)(2,1)}, f32[128,256]{1,0:T(8,128)S(1)}) custom-call(bf16[128,2304]{1,0:T(8,128)(2,1)S(1)} %bitcast.2, bf16[128,256]{1,0:T(8,128)(2,1)S(1)} %get-tuple-element.10.ordered.pre, bf16[256,2304]{1,0:T(8,128)(2,1)S(1)} %copy-done), custom_call_target="tpu_custom_call" | custom-call | flops 150994944 | bytes 1179648 | tf_op jit(solution)/shard_map/near_products/pallas_call | solution.py:208
  70.7 0.3 collective-permute-done.1.other
  71.0 1.9 %last_products.1 = (bf16[256,2304]{1,0:T(8,128)(2,1)}, bf16[2304,256]{1,0:T(8,128)(2,1)}) custom-call(bf16[128,2304]{1,0:T(8,128)(2,1)S(1)} %bitcast.3, bf16[128,2304]{1,0:T(8,128)(2,1)S(1)} %collective-permute-done.1.other, bf16[128,256]{1,0:T(8,128)(2,1)S(1)} %get-tuple-element.10.ordered.pre, ...), custom_call_target="tpu_custom_call", output_to_operand_aliasing={{0}: (5, {})} | custom-call | tf_op jit(solution)/shard_map/last_products/pallas_call | solution.py:285
Async XLA Ops:
  2.3 10.3 %collective-permute-start = (bf16[128,1152]{1,0:T(8,128)(2,1)S(1)}, bf16[128,1152]{1,0:T(8,128)(2,1)S(1)}, u32[]{:S(2)}, u32[]{:S(2)}) collective-permute-start(bf16[128,1152]{1,0:T(8,128)(2,1)S(1)} %get-tuple-element.12), channel_id=1, source_target_pairs={{0,32},{32,0},{1,33},{33,1},{2,34},{34,2},{3,35},{35,3},{4,36},{36... | collective-permute-start | bytes 884744 | tf_op jit(solution)/shard_map/ppermute | solution.py:316
  47.5 22.0 %copy-start = (bf16[256,2304]{1,0:T(8,128)(2,1)S(1)}, bf16[256,2304]{1,0:T(8,128)(2,1)}, u32[]{:S(2)}) copy-start(bf16[256,2304]{1,0:T(8,128)(2,1)} %weight.3) | copy-start | bytes 3538948
  65.5 5.6 %collective-permute-start.1 = (bf16[128,2304]{1,0:T(8,128)(2,1)S(1)}, bf16[128,2304]{1,0:T(8,128)(2,1)S(1)}, u32[]{:S(2)}, u32[]{:S(2)}) collective-permute-start(bf16[128,2304]{1,0:T(8,128)(2,1)S(1)} %bitcast.1), channel_id=1, source_target_pairs={{0,32},{32,0},{1,33},{33,1},{2,34},{34,2},{3,35},{35,3},{4,36},{36... | collective-permute-start | bytes 1769480 | tf_op jit(solution)/shard_map/ppermute | solution.py:325

commit v6 on v5

--- a/solution.py
+++ b/solution.py
@@ -59,10 +59,13 @@
         columns_there = pl.ds(pl.multiple_of(there + i * step, LANES), step)
         pairs.append((weight_hbm.at[:, columns_there], weight.at[:, pl.ds(i * step, step)]))
     copies = [pltpu.make_async_copy(a, b, sems.at[i]) for i, (a, b) in enumerate(pairs)]
-    for copy in copies:
+    for copy in copies[2:] + copies[:2]:
         copy.start()
     order = row_order(batch, rows)
     first = ((x * 2 + yh) * 2 + core) * columns
+    copies[2].wait()
+    ordered[...] = dot(order, pre[...], (1, 0)).astype(BF16)
+    hidden = jnp.maximum(ordered[...], jnp.zeros_like(ordered[...]))
     copies[0].wait()
     copies[1].wait()
     whole = bias[...].reshape(1, width)
@@ -74,9 +77,6 @@
     line = jnp.concatenate([mine, jnp.zeros((rows, half - columns), F32)], axis=1)
     line = jnp.concatenate([line, jnp.zeros((piece - rows, half), F32)], axis=0)
     strip[...] = pltpu.roll(pltpu.roll(line, lax.rem(first, half), 1), ya * rows, 0)
-    copies[2].wait()
-    ordered[...] = dot(order, pre[...], (1, 0)).astype(BF16)
-    hidden = jnp.maximum(ordered[...], jnp.zeros_like(ordered[...]))
     place = jnp.where(first // half == core, batch, (za * 2 + yb) * 2 + zb)
     for i in range(CHUNKS):
         copies[3 + i].wait()
@@ -190,27 +190,57 @@
         out[i] = payload
 
 
-def near_kernel(own, pre, weight, decoder_out, backward, decoder, sem):
-    half = decoder.shape[1]
+def tail_rows(source, half, tail):
+    xs, yhs, zas = (lax.axis_size(a) for a in ("x", "yh", "za"))
+    depth = source.shape[0] // zas
+    lane = lax.broadcasted_iota(jnp.int32, (depth, LANES), 1) // (yhs * tail)
+    pieces = [
+        source[x * depth : (x + 1) * depth, half + zas * yhs * LANES :].astype(F32)
+        for x in range(xs)
+    ]
+    blocks = []
+    for za in range(zas):
+        block = jnp.zeros((depth, LANES), F32)
+        for x in range(xs):
+            shift = (x - za) * yhs * tail % LANES
+            moved = pltpu.roll(pieces[x], shift, 1) if shift else pieces[x]
+            block = jnp.where(lane == x, moved, block)
+        blocks.append(block.astype(BF16))
+    return jnp.concatenate(blocks, axis=0)
+
+
+def near_kernel(tail, own, pre, weight, decoder_out, backward, tails, decoder, sems):
+    features, half = decoder.shape
     core = lax.axis_index("core")
     hidden = jnp.maximum(pre[...], jnp.zeros_like(pre[...]))
     columns = pl.ds(pl.multiple_of(core * half, LANES), half)
-    decoder[...] = dot(hidden, own[:, :half], (0, 0)).astype(BF16)
-    copy = pltpu.make_async_copy(decoder, decoder_out.at[:, columns], sem)
-    copy.start()
+    copies = []
+    for i in range(2):
+        part = slice(i * features // 2, (i + 1) * features // 2)
+        decoder[part, :] = dot(hidden[:, part], own[:, :half], (0, 0)).astype(BF16)
+        copies.append(
+            pltpu.make_async_copy(decoder.at[part], decoder_out.at[part, columns], sems.at[i])
+        )
+        copies[-1].start()
     backward[...] = dot(own[:, :half], weight[:, columns], (1, 1))
-    copy.wait()
-
-
-def near_products(own, pre, weight):
+    tails[...] = tail_rows(own, half, tail)
+    for copy in copies:
+        copy.wait()
+
+
+def near_products(own, pre, weight, tail):
     features, width = weight.shape
     half = width // lax.axis_size("core")
     return pl.pallas_call(
-        near_kernel,
-        out_shape=(pltpu.HBM((features, width), BF16), pltpu.VMEM(pre.shape, F32)),
+        functools.partial(near_kernel, tail),
+        out_shape=(
+            pltpu.HBM((features, width), BF16),
+            pltpu.VMEM(pre.shape, F32),
+            pltpu.VMEM((pre.shape[0], LANES), BF16),
+        ),
         in_specs=[VMEM] * 3,
-        out_specs=(pl.BlockSpec(memory_space=pltpu.HBM), VMEM),
-        scratch_shapes=[pltpu.VMEM((features, half), BF16), pltpu.SemaphoreType.DMA],
+        out_specs=(pl.BlockSpec(memory_space=pltpu.HBM), VMEM, VMEM),
+        scratch_shapes=[pltpu.VMEM((features, half), BF16), pltpu.SemaphoreType.DMA((2,))],
         compiler_params=pltpu.CompilerParams(vmem_limit_bytes=10 << 20),
         cost_estimate=pl.CostEstimate(
             flops=4 * pre.shape[0] * features * half,
@@ -222,44 +252,33 @@
 
 
 def last_kernel(
-    tail, own, other, pre, weight, backward, _, decoder_out, encoder_out, decoder, encoder, sems
+    tail, own, other, pre, weight, backward, tails, _, decoder_out, encoder_out, decoder, encoder, sems
 ):
-    batch, half = other.shape[0], decoder.shape[1]
+    batch, (features, half) = other.shape[0], decoder.shape
     core = lax.axis_index("core")
     cores, xs, yhs, zas = (lax.axis_size(a) for a in ("core", "x", "yh", "za"))
     depth, span = batch // zas, LANES + tail
     sources = ((own, core), (other, 1 - core))
+    columns = pl.ds(pl.multiple_of((1 - core) * half, LANES), half)
     copies = []
-
-    def send(source, target):
-        copies.append(pltpu.make_async_copy(source, target, sems.at[len(copies)]))
-        copies[-1].start()
-
-    columns = pl.ds(pl.multiple_of((1 - core) * half, LANES), half)
-    residual = other[:, :half]
-    total = backward[...] + dot(residual, weight[:, columns], (1, 1))
+    for i in range(2):
+        part = slice(i * features // 2, (i + 1) * features // 2)
+        copies.append(
+            pltpu.make_async_copy(decoder.at[part], decoder_out.at[part, columns], sems.at[i])
+        )
+
+    @pl.when(core < cores)
+    def _():
+        hidden = jnp.maximum(pre[...], jnp.zeros_like(pre[...]))
+        for i in range(2):
+            part = slice(i * features // 2, (i + 1) * features // 2)
+            decoder[part, :] = dot(hidden[:, part], other[:, :half], (0, 0)).astype(BF16)
+            copies[i].start()
+
+    total = backward[...] + dot(other[:, :half], weight[:, columns], (1, 1))
     masked = jnp.where(pre[...] > 0, total, jnp.zeros_like(total)).astype(BF16)
-    hidden = jnp.maximum(pre[...], jnp.zeros_like(pre[...]))
-    decoder[...] = dot(hidden, residual, (0, 0)).astype(BF16)
-    send(decoder, decoder_out.at[:, columns])
-
-    lane = lax.broadcasted_iota(jnp.int32, (depth, LANES), 1) // (yhs * tail)
-    ends = []
-    for source, _ in sources:
-        pieces = [
-            source[x * depth : (x + 1) * depth, half + zas * yhs * LANES :].astype(F32)
-            for x in range(xs)
-        ]
-        blocks = []
-        for za in range(zas):
-            block = jnp.zeros((depth, LANES), F32)
-            for x in range(xs):
-                shift = (x - za) * yhs * tail % LANES
-                moved = pltpu.roll(pieces[x], shift, 1) if shift else pieces[x]
-                block = jnp.where(lane == x, moved, block)
-            blocks.append(block.astype(BF16))
-        ends.append(dot(jnp.concatenate(blocks, axis=0), masked, (0, 0)).astype(BF16))
-
+    rows = (tails[...], tail_rows(other, half, tail))
+    ends = [dot(r, masked, (0, 0)).astype(BF16) for r in rows]
     for x in range(xs):
         for k, (source, c) in enumerate(sources):
             size = yhs * LANES
@@ -274,12 +293,15 @@
                 end = (x * yhs + yh) * tail
                 encoder[pl.ds(pl.multiple_of(start + LANES, tail), tail), :] = ends[k][end : end + tail]
         block = pl.ds(x * yhs * cores * span, yhs * cores * span)
-        send(encoder.at[block], encoder_out.at[block])
+        copies.append(
+            pltpu.make_async_copy(encoder.at[block], encoder_out.at[block], sems.at[len(copies)])
+        )
+        copies[-1].start()
     for copy in copies:
         copy.wait()
 
 
-def last_products(own, other, pre, weight, backward, decoder, tail):
+def last_products(own, other, pre, weight, backward, tails, decoder, tail):
     features, width = weight.shape
     raw = pl.BlockSpec(memory_space=pltpu.HBM)
     return pl.pallas_call(
@@ -288,17 +310,17 @@
             jax.ShapeDtypeStruct((features, width), BF16),
             jax.ShapeDtypeStruct((width, features), BF16),
         ),
-        in_specs=[VMEM] * 5 + [raw],
+        in_specs=[VMEM] * 6 + [raw],
         out_specs=(raw, raw),
         scratch_shapes=[
             pltpu.VMEM((features, width // lax.axis_size("core")), BF16),
             pltpu.VMEM((width, features), BF16),
-            pltpu.SemaphoreType.DMA((1 + lax.axis_size("x"),)),
+            pltpu.SemaphoreType.DMA((2 + lax.axis_size("x"),)),
         ],
-        input_output_aliases={5: 0},
+        input_output_aliases={6: 0},
         compiler_params=pltpu.CompilerParams(vmem_limit_bytes=20 << 20),
         name="last_products",
-    )(own, other, pre, weight, backward, decoder)
+    )(own, other, pre, weight, backward, tails, decoder)
 
 
 def shards(inputs, decoder_bias, preactivations, decoder_weight):
@@ -323,9 +345,9 @@
     kernel = functools.partial(third_kernel, half, tail)
     own = swap(small_kernel(kernel, shape, 8, "third_sum", arrived), NEAR).reshape(batch, width)
     other = lax.ppermute(own, "core", partner)
-    decoder, backward = near_products(own, ordered, decoder_weight)
+    decoder, backward, tails = near_products(own, ordered, decoder_weight, tail)
     grad_decoder, grad_encoder = last_products(
-        own, other, ordered, decoder_weight, backward, decoder, tail
+        own, other, ordered, decoder_weight, backward, tails, decoder, tail
     )
     return (grad_encoder, grad_decoder)
 

time: 73.2 us -> 73.7 us (level)
  no operation moved by 1% of the time
where the time goes in v6:
time: 73.7 us; the launch traced here: 73.4 us
  blocking collectives  52.6 us (71%)
  starting transfers between devices  12.7 us (17%)
  Pallas kernels  6.91 us (9%)
    all_to_all x3, blocking collectives, swap(): return lax.all_to_all(x, axis, split_axis=0, concat_axis=0, tiled=True)  52.6 us
    ppermute x1, starting transfers between devices, shards(): arrived = lax.ppermute(theirs, 'core', partner)  8.75 us
    ppermute x1, starting transfers between devices, shards(): other = lax.ppermute(own, 'core', partner)  3.94 us
    pallas_call x1, Pallas kernels, last_products(): pl.pallas_call(functools.partial(last_kernel, tail), out_shape=(jax.Shape...  2.22 us
    pallas_call x1, Pallas kernels, first_product(): pl.pallas_call(first_kernel, out_shape=(pltpu.VMEM((pre.shape[0], half),...  1.84 us
    pallas_call x1, Pallas kernels, own_product(): pl.pallas_call(own_kernel, out_shape=pltpu.VMEM((batch, half), F32), in_s...  1.54 us
  transfers between devices with their start and end apart: 2, of which 1 were waited for; matrix products, arithmetic and copies ran while one was open for 0% of the time, Pallas kernels for 4%

profile of v6, /device:TPU:1, one launch (start us, length us, event | category | flops | bytes accessed | tf_op | source)
XLA Modules:
  0.0 73.4 jit_solution(15147460226829316965)
XLA Ops:
  0.6 1.8 %first_product.1 = (bf16[128,1152]{1,0:T(8,128)(2,1)S(1)}, bf16[128,256]{1,0:T(8,128)(2,1)S(1)}, bf16[8,128]{1,0:T(8,128)(2,1)S(1)}, f32[8,1152]{1,0:T(8,128)S(1)}) custom-call(bf16[128,256]{1,0:T(8,128)(2,1)} %pre_hbm.1, bf16[256,2304]{1,0:T(8,128)(2,1)} %weight.3, bf16[4,144]{1,0:T(4,128)(2,1)} %inputs_hbm.1, f32[2304]{0:T(1024)} %bias_hbm.1), custom_call_target="tpu_custom_call" | custom-call | tf_op jit(solution)/shard_map/first_product/pallas_call | solution.py:99
  2.5 8.7 %collective-permute-start = (bf16[128,1152]{1,0:T(8,128)(2,1)S(1)}, bf16[128,1152]{1,0:T(8,128)(2,1)S(1)}, u32[]{:S(2)}, u32[]{:S(2)}) collective-permute-start(bf16[128,1152]{1,0:T(8,128)(2,1)S(1)} %get-tuple-element.13), channel_id=1, source_target_pairs={{0,32},{32,0},{1,33},{33,1},{2,34},{34,2},{3,35},{35,3},{4,36},{36... | collective-permute-start | bytes 884744 | tf_op jit(solution)/shard_map/ppermute | solution.py:338
  11.2 1.5 %own_product.1.own = f32[128,1152]{1,0:T(8,128)S(1)} custom-call(bf16[128,256]{1,0:T(8,128)(2,1)S(1)} %get-tuple-element.11.ordered.pre, f32[8,1152]{1,0:T(8,128)S(1)} %get-tuple-element.12.strip, bf16[256,2304]{1,0:T(8,128)(2,1)} %weight.3), custom_call_target="tpu_custom_call" | custom-call | flops 75497472 | bytes 589824 | tf_op jit(solution)/shard_map/own_product/pallas_call | solution.py:143
  12.8 0.0 collective-permute-done.arrived
  12.8 0.1 join_cores.1
  12.9 10.2 %all_to_all.15.arrived = bf16[16,8,1152]{2,1,0:T(8,128)(2,1)S(1)} all-to-all(bf16[16,8,1152]{2,1,0:T(8,128)(2,1)S(1)} %join_cores.1), channel_id=1, replica_groups=mesh['x'=4,'yh'=2,'core'=2,'ya'=2,'yb'=2,'za'=4,'zb'=2] {'x','yb','zb'}, dimensions={0} | all-to-all | bytes 589824 | tf_op jit(solution)/shard_map/all_to_all | solution.py:19
  23.1 0.1 second_sum.1
  23.1 24.5 %all_to_all.16.arrived = bf16[16,8,1280]{2,1,0:T(8,128)(2,1)S(1)} all-to-all(bf16[16,8,1280]{2,1,0:T(8,128)(2,1)S(1)} %second_sum.1), channel_id=1, replica_groups=mesh['x'=4,'yh'=2,'core'=2,'ya'=2,'yb'=2,'za'=4,'zb'=2] {'yh','ya','za'}, dimensions={0} | all-to-all | bytes 655360 | tf_op jit(solution)/shard_map/all_to_all | solution.py:19
  47.6 0.0 copy-start
  47.6 0.1 third_sum.1
  47.7 17.9 %all_to_all.17 = bf16[16,8,2304]{2,1,0:T(8,128)(2,1)S(1)} all-to-all(bf16[16,8,2304]{2,1,0:T(8,128)(2,1)S(1)} %third_sum.1), channel_id=1, replica_groups=mesh['x'=4,'yh'=2,'core'=2,'ya'=2,'yb'=2,'za'=4,'zb'=2] {'x','yb','zb'}, dimensions={0} | all-to-all | bytes 1179648 | tf_op jit(solution)/shard_map/all_to_all | solution.py:19
  65.6 3.9 %collective-permute-start.1 = (bf16[128,2304]{1,0:T(8,128)(2,1)S(1)}, bf16[128,2304]{1,0:T(8,128)(2,1)S(1)}, u32[]{:S(2)}, u32[]{:S(2)}) collective-permute-start(bf16[128,2304]{1,0:T(8,128)(2,1)S(1)} %bitcast.1), channel_id=1, source_target_pairs={{0,32},{32,0},{1,33},{33,1},{2,34},{34,2},{3,35},{35,3},{4,36},{36... | collective-permute-start | bytes 1769480 | tf_op jit(solution)/shard_map/ppermute | solution.py:347
  69.6 0.0 copy-done
  69.6 1.1 %near_products.1 = (bf16[256,2304]{1,0:T(8,128)(2,1)}, f32[128,256]{1,0:T(8,128)S(1)}, bf16[128,128]{1,0:T(8,128)(2,1)S(1)}) custom-call(bf16[128,2304]{1,0:T(8,128)(2,1)S(1)} %bitcast.2, bf16[128,256]{1,0:T(8,128)(2,1)S(1)} %get-tuple-element.11.ordered.pre, bf16[256,2304]{1,0:T(8,128)(2,1)S(1)} %copy-done), custom_call_target="tpu_custom_call" | custom-call | flops 150994944 | bytes 1179648 | tf_op jit(solution)/shard_map/near_products/pallas_call | solution.py:234
  70.7 0.5 collective-permute-done.1.other
  71.2 2.2 %last_products.1 = (bf16[256,2304]{1,0:T(8,128)(2,1)}, bf16[2304,256]{1,0:T(8,128)(2,1)}) custom-call(bf16[128,2304]{1,0:T(8,128)(2,1)S(1)} %bitcast.3, bf16[128,2304]{1,0:T(8,128)(2,1)S(1)} %collective-permute-done.1.other, bf16[128,256]{1,0:T(8,128)(2,1)S(1)} %get-tuple-element.11.ordered.pre, ...), custom_call_target="tpu_custom_call", output_to_operand_aliasing={{0}: (6, {})} | custom-call | tf_op jit(solution)/shard_map/last_products/pallas_call | solution.py:307
Async XLA Ops:
  2.5 10.3 %collective-permute-start = (bf16[128,1152]{1,0:T(8,128)(2,1)S(1)}, bf16[128,1152]{1,0:T(8,128)(2,1)S(1)}, u32[]{:S(2)}, u32[]{:S(2)}) collective-permute-start(bf16[128,1152]{1,0:T(8,128)(2,1)S(1)} %get-tuple-element.13), channel_id=1, source_target_pairs={{0,32},{32,0},{1,33},{33,1},{2,34},{34,2},{3,35},{35,3},{4,36},{36... | collective-permute-start | bytes 884744 | tf_op jit(solution)/shard_map/ppermute | solution.py:338
  47.6 22.0 %copy-start = (bf16[256,2304]{1,0:T(8,128)(2,1)S(1)}, bf16[256,2304]{1,0:T(8,128)(2,1)}, u32[]{:S(2)}) copy-start(bf16[256,2304]{1,0:T(8,128)(2,1)} %weight.3) | copy-start | bytes 3538948
  65.6 5.6 %collective-permute-start.1 = (bf16[128,2304]{1,0:T(8,128)(2,1)S(1)}, bf16[128,2304]{1,0:T(8,128)(2,1)S(1)}, u32[]{:S(2)}, u32[]{:S(2)}) collective-permute-start(bf16[128,2304]{1,0:T(8,128)(2,1)S(1)} %bitcast.1), channel_id=1, source_target_pairs={{0,32},{32,0},{1,33},{33,1},{2,34},{34,2},{3,35},{35,3},{4,36},{36... | collective-permute-start | bytes 1769480 | tf_op jit(solution)/shard_map/ppermute | solution.py:347

commit v7 on v6

--- a/solution.py
+++ b/solution.py
@@ -12,11 +12,28 @@
 AXES = ("x", "yh", "core", "ya", "yb", "za", "zb")
 SIZES = (4, 2, 2, 2, 2, 4, 2)
 NEAR, FAR = ("x", "yb", "zb"), ("yh", "ya", "za")
+PLANE = ("yh", "ya", "yb", "za", "zb")
 VMEM = pl.BlockSpec(memory_space=pltpu.VMEM)
 
 
-def swap(x, axis):
-    return lax.all_to_all(x, axis, split_axis=0, concat_axis=0, tiled=True)
+def members(xs, ys, zs):
+    return [(x * 8 + y) * 8 + z for x in xs for y in ys for z in zs]
+
+
+def near_groups():
+    pairs = [sorted((2 * k, 2 * k + 1), key=parity) for k in range(4)]
+    return [members(range(4), ys, zs) for ys in pairs for zs in pairs]
+
+
+def far_groups():
+    sets = [[n for n in range(8) if parity(n) == side] for side in range(2)]
+    return [members((0,), ys, zs) for ys in sets for zs in sets]
+
+
+def swap(x, axis, groups):
+    return lax.all_to_all(
+        x, axis, split_axis=0, concat_axis=0, axis_index_groups=groups, tiled=True
+    )
 
 
 def dot(a, b, contract):
@@ -34,6 +51,14 @@
     )(*operands)
 
 
+def parity(n):
+    return (n ^ (n >> 1) ^ (n >> 2)) & 1
+
+
+def own_place(ya, yb, za, zb):
+    return (za * 2 + (yb ^ ya)) * 2 + (zb ^ parity(za))
+
+
 def row_order(batch, rows):
     shape = (batch, batch)
     new = lax.broadcasted_iota(jnp.int32, shape, 0)
@@ -41,6 +66,7 @@
     ya, group = lax.rem(group, 2), group // 2
     zb, group = lax.rem(group, 2), group // 2
     yb, za = lax.rem(group, 2), group // 2
+    yb, zb = yb ^ ya, zb ^ parity(za)
     old = ((((ya * 2 + yb) * 4 + za) * 2) + zb) * rows + r
     return jnp.where(lax.broadcasted_iota(jnp.int32, shape, 1) == old, 1.0, 0.0).astype(BF16)
 
@@ -59,13 +85,10 @@
         columns_there = pl.ds(pl.multiple_of(there + i * step, LANES), step)
         pairs.append((weight_hbm.at[:, columns_there], weight.at[:, pl.ds(i * step, step)]))
     copies = [pltpu.make_async_copy(a, b, sems.at[i]) for i, (a, b) in enumerate(pairs)]
-    for copy in copies[2:] + copies[:2]:
+    for copy in copies:
         copy.start()
     order = row_order(batch, rows)
     first = ((x * 2 + yh) * 2 + core) * columns
-    copies[2].wait()
-    ordered[...] = dot(order, pre[...], (1, 0)).astype(BF16)
-    hidden = jnp.maximum(ordered[...], jnp.zeros_like(ordered[...]))
     copies[0].wait()
     copies[1].wait()
     whole = bias[...].reshape(1, width)
@@ -77,7 +100,10 @@
     line = jnp.concatenate([mine, jnp.zeros((rows, half - columns), F32)], axis=1)
     line = jnp.concatenate([line, jnp.zeros((piece - rows, half), F32)], axis=0)
     strip[...] = pltpu.roll(pltpu.roll(line, lax.rem(first, half), 1), ya * rows, 0)
-    place = jnp.where(first // half == core, batch, (za * 2 + yb) * 2 + zb)
+    copies[2].wait()
+    ordered[...] = dot(order, pre[...], (1, 0)).astype(BF16)
+    hidden = jnp.maximum(ordered[...], jnp.zeros_like(ordered[...]))
+    place = jnp.where(first // half == core, batch, own_place(ya, yb, za, zb))
     for i in range(CHUNKS):
         copies[3 + i].wait()
         part = pl.ds(i * step, step)
@@ -129,7 +155,7 @@
         copies.append(pltpu.make_async_copy(weight_hbm.at[:, columns], target, sems.at[i]))
         copies[-1].start()
     hidden = jnp.maximum(ordered[...], jnp.zeros_like(ordered[...]))
-    place = jnp.where(x * 2 // lax.axis_size("x") == core, (za * 2 + yb) * 2 + zb, batch)
+    place = jnp.where(x * 2 // lax.axis_size("x") == core, own_place(ya, yb, za, zb), batch)
     for i in range(CHUNKS):
         copies[i].wait()
         part = pl.ds(i * step, step)
@@ -209,41 +235,56 @@
     return jnp.concatenate(blocks, axis=0)
 
 
-def near_kernel(tail, own, pre, weight, decoder_out, backward, tails, decoder, sems):
+def block_rows(source, x, half):
+    yhs, zas = lax.axis_size("yh"), lax.axis_size("za")
+    depth, size = source.shape[0] // zas, yhs * LANES
+    part = [
+        source[x * depth : (x + 1) * depth, half + za * size : half + (za + 1) * size]
+        for za in range(zas)
+    ]
+    return jnp.concatenate(part, axis=0)
+
+
+def near_kernel(tail, own, pre, weight, decoder_out, backward, turned, flipped, decoder, sems):
     features, half = decoder.shape
     core = lax.axis_index("core")
-    hidden = jnp.maximum(pre[...], jnp.zeros_like(pre[...]))
+    xs, size = lax.axis_size("x"), lax.axis_size("yh") * LANES
+    flipped[...] = jnp.maximum(pre[...], jnp.zeros_like(pre[...])).T
     columns = pl.ds(pl.multiple_of(core * half, LANES), half)
     copies = []
     for i in range(2):
         part = slice(i * features // 2, (i + 1) * features // 2)
-        decoder[part, :] = dot(hidden[:, part], own[:, :half], (0, 0)).astype(BF16)
+        decoder[part, :] = dot(flipped[part, :], own[:, :half], (1, 0)).astype(BF16)
         copies.append(
             pltpu.make_async_copy(decoder.at[part], decoder_out.at[part, columns], sems.at[i])
         )
         copies[-1].start()
     backward[...] = dot(own[:, :half], weight[:, columns], (1, 1))
-    tails[...] = tail_rows(own, half, tail)
+    for x in range(xs):
+        turned[x * size : (x + 1) * size, :] = block_rows(own, x, half).T
+    turned[xs * size :, :] = tail_rows(own, half, tail).T
     for copy in copies:
         copy.wait()
 
 
 def near_products(own, pre, weight, tail):
     features, width = weight.shape
+    batch = pre.shape[0]
     half = width // lax.axis_size("core")
     return pl.pallas_call(
         functools.partial(near_kernel, tail),
         out_shape=(
             pltpu.HBM((features, width), BF16),
             pltpu.VMEM(pre.shape, F32),
-            pltpu.VMEM((pre.shape[0], LANES), BF16),
+            pltpu.VMEM((half, batch), BF16),
+            pltpu.VMEM((features, batch), BF16),
         ),
         in_specs=[VMEM] * 3,
-        out_specs=(pl.BlockSpec(memory_space=pltpu.HBM), VMEM, VMEM),
+        out_specs=(pl.BlockSpec(memory_space=pltpu.HBM), VMEM, VMEM, VMEM),
         scratch_shapes=[pltpu.VMEM((features, half), BF16), pltpu.SemaphoreType.DMA((2,))],
         compiler_params=pltpu.CompilerParams(vmem_limit_bytes=10 << 20),
         cost_estimate=pl.CostEstimate(
-            flops=4 * pre.shape[0] * features * half,
+            flops=4 * batch * features * half,
             bytes_accessed=features * width * 2,
             transcendentals=0,
         ),
@@ -252,56 +293,52 @@
 
 
 def last_kernel(
-    tail, own, other, pre, weight, backward, tails, _, decoder_out, encoder_out, decoder, encoder, sems
+    tail, other, pre, weight, backward, turned, flipped, _, decoder_out, encoder_out, decoder, encoder, sems
 ):
-    batch, (features, half) = other.shape[0], decoder.shape
+    half = decoder.shape[1]
     core = lax.axis_index("core")
-    cores, xs, yhs, zas = (lax.axis_size(a) for a in ("core", "x", "yh", "za"))
-    depth, span = batch // zas, LANES + tail
-    sources = ((own, core), (other, 1 - core))
+    cores, xs, yhs = (lax.axis_size(a) for a in ("core", "x", "yh"))
+    span, size = LANES + tail, yhs * LANES
+    copies = []
+
+    def send(source, target):
+        copies.append(pltpu.make_async_copy(source, target, sems.at[len(copies)]))
+        copies[-1].start()
+
     columns = pl.ds(pl.multiple_of((1 - core) * half, LANES), half)
-    copies = []
-    for i in range(2):
-        part = slice(i * features // 2, (i + 1) * features // 2)
-        copies.append(
-            pltpu.make_async_copy(decoder.at[part], decoder_out.at[part, columns], sems.at[i])
-        )
-
-    @pl.when(core < cores)
-    def _():
-        hidden = jnp.maximum(pre[...], jnp.zeros_like(pre[...]))
-        for i in range(2):
-            part = slice(i * features // 2, (i + 1) * features // 2)
-            decoder[part, :] = dot(hidden[:, part], other[:, :half], (0, 0)).astype(BF16)
-            copies[i].start()
-
-    total = backward[...] + dot(other[:, :half], weight[:, columns], (1, 1))
+    residual = other[:, :half]
+    total = backward[...] + dot(residual, weight[:, columns], (1, 1))
     masked = jnp.where(pre[...] > 0, total, jnp.zeros_like(total)).astype(BF16)
-    rows = (tails[...], tail_rows(other, half, tail))
-    ends = [dot(r, masked, (0, 0)).astype(BF16) for r in rows]
+    decoder[...] = dot(flipped[...], residual, (1, 0)).astype(BF16)
+    send(decoder, decoder_out.at[:, columns])
+    depth = masked.shape[0] // (2 * lax.axis_size("za"))
+    swapped = [masked[(i ^ 1) * depth : ((i ^ 1) + 1) * depth] for i in range(masked.shape[0] // depth)]
+    met = (masked, jnp.concatenate(swapped, axis=0))
+    other_tails = tail_rows(other, half, tail)
+    own_ends = [dot(turned[xs * size :, :], m, (1, 0)).astype(BF16) for m in met]
+    other_ends = [dot(other_tails, m, (0, 0)).astype(BF16) for m in met]
     for x in range(xs):
-        for k, (source, c) in enumerate(sources):
-            size = yhs * LANES
-            part = [
-                source[x * depth : (x + 1) * depth, half + za * size : half + (za + 1) * size]
-                for za in range(zas)
-            ]
-            product = dot(jnp.concatenate(part, axis=0), masked, (0, 0)).astype(BF16)
-            for yh in range(yhs):
+        theirs = block_rows(other, x, half)
+        for yh, m in enumerate(met):
+            first = x * size + yh * LANES
+            own_block = dot(turned[first : first + LANES, :], m, (1, 0)).astype(BF16)
+            other_block = dot(theirs[:, yh * LANES : (yh + 1) * LANES], m, (0, 0)).astype(BF16)
+            end = (x * yhs + yh) * tail
+            for block, ends, c in (
+                (own_block, own_ends[yh], core),
+                (other_block, other_ends[yh], 1 - core),
+            ):
                 start = pl.multiple_of(((x * yhs + yh) * cores + c) * span, tail)
-                encoder[pl.ds(start, LANES), :] = product[yh * LANES : (yh + 1) * LANES]
-                end = (x * yhs + yh) * tail
-                encoder[pl.ds(pl.multiple_of(start + LANES, tail), tail), :] = ends[k][end : end + tail]
-        block = pl.ds(x * yhs * cores * span, yhs * cores * span)
-        copies.append(
-            pltpu.make_async_copy(encoder.at[block], encoder_out.at[block], sems.at[len(copies)])
-        )
-        copies[-1].start()
+                encoder[pl.ds(start, LANES), :] = block
+                encoder[pl.ds(pl.multiple_of(start + LANES, tail), tail), :] = ends[end : end + tail]
+        rows = pl.ds(x * yhs * cores * span, yhs * cores * span)
+        send(encoder.at[rows], encoder_out.at[rows])
     for copy in copies:
         copy.wait()
 
 
-def last_products(own, other, pre, weight, backward, tails, decoder, tail):
+def last_products(other, pre, weight, near, tail):
+    decoder, *rest = near
     features, width = weight.shape
     raw = pl.BlockSpec(memory_space=pltpu.HBM)
     return pl.pallas_call(
@@ -315,12 +352,12 @@
         scratch_shapes=[
             pltpu.VMEM((features, width // lax.axis_size("core")), BF16),
             pltpu.VMEM((width, features), BF16),
-            pltpu.SemaphoreType.DMA((2 + lax.axis_size("x"),)),
+            pltpu.SemaphoreType.DMA((1 + lax.axis_size("x"),)),
         ],
         input_output_aliases={6: 0},
         compiler_params=pltpu.CompilerParams(vmem_limit_bytes=20 << 20),
         name="last_products",
-    )(own, other, pre, weight, backward, tails, decoder)
+    )(other, pre, weight, *rest, decoder)
 
 
 def shards(inputs, decoder_bias, preactivations, decoder_weight):
@@ -338,17 +375,16 @@
     arrived = lax.ppermute(theirs, "core", partner)
     mine = own_product(ordered, strip, decoder_weight)
     shape = jax.ShapeDtypeStruct((near, piece, half), BF16)
-    arrived = swap(small_kernel(join_kernel, shape, 8, "join_cores", mine, arrived), NEAR)
+    arrived = swap(small_kernel(join_kernel, shape, 8, "join_cores", mine, arrived), ("x", *PLANE), near_groups())
     shape = jax.ShapeDtypeStruct((far, piece, half + LANES), BF16)
-    arrived = swap(small_kernel(second_kernel, shape, 8, "second_sum", arrived, tile), FAR)
+    arrived = swap(small_kernel(second_kernel, shape, 8, "second_sum", arrived, tile), PLANE, far_groups())
     shape = jax.ShapeDtypeStruct((near, piece, width), BF16)
     kernel = functools.partial(third_kernel, half, tail)
-    own = swap(small_kernel(kernel, shape, 8, "third_sum", arrived), NEAR).reshape(batch, width)
+    own = small_kernel(kernel, shape, 8, "third_sum", arrived)
+    own = swap(own, ("x", *PLANE), near_groups()).reshape(batch, width)
     other = lax.ppermute(own, "core", partner)
-    decoder, backward, tails = near_products(own, ordered, decoder_weight, tail)
-    grad_decoder, grad_encoder = last_products(
-        own, other, ordered, decoder_weight, backward, tails, decoder, tail
-    )
+    near_part = near_products(own, ordered, decoder_weight, tail)
+    grad_decoder, grad_encoder = last_products(other, ordered, decoder_weight, near_part, tail)
     return (grad_encoder, grad_decoder)
 
 

time: 73.7 us -> 71.7 us (0.973)
  blocking collectives: 52.6 us -> 50.3 us
    all_to_all x3, blocking collectives: 52.6 us -> 50.3 us  [swap(): lax.all_to_all(x, axis, split_axis=0, concat_axis=0, axis_index_groups=gr...]
where the time goes in v7:
time: 71.7 us; the launch traced here: 71.4 us
  blocking collectives  50.3 us (70%)
  starting transfers between devices  13.4 us (19%)
  Pallas kernels  6.51 us (9%)
    all_to_all x3, blocking collectives, swap(): lax.all_to_all(x, axis, split_axis=0, concat_axis=0, axis_index_groups=gr...  50.3 us
    ppermute x1, starting transfers between devices, shards(): arrived = lax.ppermute(theirs, 'core', partner)  8.75 us
    ppermute x1, starting transfers between devices, shards(): other = lax.ppermute(own, 'core', partner)  4.66 us
    pallas_call x1, Pallas kernels, last_products(): pl.pallas_call(functools.partial(last_kernel, tail), out_shape=(jax.Shape...  1.92 us
    pallas_call x1, Pallas kernels, first_product(): pl.pallas_call(first_kernel, out_shape=(pltpu.VMEM((pre.shape[0], half),...  1.69 us
    pallas_call x1, Pallas kernels, own_product(): pl.pallas_call(own_kernel, out_shape=pltpu.VMEM((batch, half), F32), in_s...  1.54 us
  transfers between devices with their start and end apart: 2, of which 1 were waited for; matrix products, arithmetic and copies ran while one was open for 0% of the time, Pallas kernels for 4%

profile of v7, /device:TPU:1, one launch (start us, length us, event | category | flops | bytes accessed | tf_op | source)
XLA Modules:
  0.0 71.4 jit_solution(11176760489875287996)
XLA Ops:
  0.6 1.7 %first_product.1 = (bf16[128,1152]{1,0:T(8,128)(2,1)S(1)}, bf16[128,256]{1,0:T(8,128)(2,1)S(1)}, bf16[8,128]{1,0:T(8,128)(2,1)S(1)}, f32[8,1152]{1,0:T(8,128)S(1)}) custom-call(bf16[128,256]{1,0:T(8,128)(2,1)} %pre_hbm.1, bf16[256,2304]{1,0:T(8,128)(2,1)} %weight.3, bf16[4,144]{1,0:T(4,128)(2,1)} %inputs_hbm.1, f32[2304]{0:T(1024)} %bias_hbm.1), custom_call_target="tpu_custom_call" | custom-call | tf_op jit(solution)/shard_map/first_product/pallas_call | solution.py:125
  2.3 8.7 %collective-permute-start = (bf16[128,1152]{1,0:T(8,128)(2,1)S(1)}, bf16[128,1152]{1,0:T(8,128)(2,1)S(1)}, u32[]{:S(2)}, u32[]{:S(2)}) collective-permute-start(bf16[128,1152]{1,0:T(8,128)(2,1)S(1)} %get-tuple-element.14), channel_id=1, source_target_pairs={{0,32},{32,0},{1,33},{33,1},{2,34},{34,2},{3,35},{35,3},{4,36},{36... | collective-permute-start | bytes 884744 | tf_op jit(solution)/shard_map/ppermute | solution.py:375
  11.1 1.5 %own_product.1.own = f32[128,1152]{1,0:T(8,128)S(1)} custom-call(bf16[128,256]{1,0:T(8,128)(2,1)S(1)} %get-tuple-element.12.ordered.pre, f32[8,1152]{1,0:T(8,128)S(1)} %get-tuple-element.13.strip, bf16[256,2304]{1,0:T(8,128)(2,1)} %weight.3), custom_call_target="tpu_custom_call" | custom-call | flops 75497472 | bytes 589824 | tf_op jit(solution)/shard_map/own_product/pallas_call | solution.py:169
  12.6 0.0 collective-permute-done.arrived
  12.6 0.1 join_cores.1
  12.7 10.2 %all_to_all.15.arrived = bf16[16,8,1152]{2,1,0:T(8,128)(2,1)S(1)} all-to-all(bf16[16,8,1152]{2,1,0:T(8,128)(2,1)S(1)} %join_cores.1), channel_id=1, replica_groups={{0,1,8,9,128,129,136,137,256,257,264,265,384,385,392,393},{3,2,11,10,13..., dimensions={0} | all-to-all | bytes 589824 | tf_op jit(solution)/shard_map/all_to_all | solution.py:34
  22.9 0.1 second_sum.1
  23.0 23.2 %all_to_all.16.arrived = bf16[16,8,1280]{2,1,0:T(8,128)(2,1)S(1)} all-to-all(bf16[16,8,1280]{2,1,0:T(8,128)(2,1)S(1)} %second_sum.1), channel_id=1, replica_groups={{0,3,5,6,24,27,29,30,72,75,77,78,80,83,85,86},{1,2,4,7,25,26,28,31,73,7..., dimensions={0} | all-to-all | bytes 655360 | tf_op jit(solution)/shard_map/all_to_all | solution.py:34
  46.2 0.0 copy-start
  46.2 0.1 third_sum.1
  46.3 16.9 %all_to_all.17 = bf16[16,8,2304]{2,1,0:T(8,128)(2,1)S(1)} all-to-all(bf16[16,8,2304]{2,1,0:T(8,128)(2,1)S(1)} %third_sum.1), channel_id=1, replica_groups={{0,1,8,9,128,129,136,137,256,257,264,265,384,385,392,393},{3,2,11,10,13..., dimensions={0} | all-to-all | bytes 1179648 | tf_op jit(solution)/shard_map/all_to_all | solution.py:34
  63.2 4.7 %collective-permute-start.1 = (bf16[128,2304]{1,0:T(8,128)(2,1)S(1)}, bf16[128,2304]{1,0:T(8,128)(2,1)S(1)}, u32[]{:S(2)}, u32[]{:S(2)}) collective-permute-start(bf16[128,2304]{1,0:T(8,128)(2,1)S(1)} %bitcast.1), channel_id=1, source_target_pairs={{0,32},{32,0},{1,33},{33,1},{2,34},{34,2},{3,35},{35,3},{4,36},{36... | collective-permute-start | bytes 1769480 | tf_op jit(solution)/shard_map/ppermute | solution.py:385
  67.9 0.0 copy-done
  67.9 1.1 %near_products.1 = (bf16[256,2304]{1,0:T(8,128)(2,1)}, f32[128,256]{1,0:T(8,128)S(1)}, bf16[1152,128]{1,0:T(8,128)(2,1)S(1)}, bf16[256,128]{1,0:T(8,128)(2,1)S(1)}) custom-call(bf16[128,2304]{1,0:T(8,128)(2,1)S(1)} %bitcast.2, bf16[128,256]{1,0:T(8,128)(2,1)S(1)} %get-tuple-element.12.ordered.pre, bf16[256,2304]{1,0:T(8,128)(2,1)S(1)} %copy-done), custom_call_target="tpu_custom_call" | custom-call | flops 150994944 | bytes 1179648 | tf_op jit(solution)/shard_map/near_products/pallas_call | solution.py:274
  69.0 0.4 collective-permute-done.1.other
  69.5 1.9 %last_products.1 = (bf16[256,2304]{1,0:T(8,128)(2,1)}, bf16[2304,256]{1,0:T(8,128)(2,1)}) custom-call(bf16[128,2304]{1,0:T(8,128)(2,1)S(1)} %collective-permute-done.1.other, bf16[128,256]{1,0:T(8,128)(2,1)S(1)} %get-tuple-element.12.ordered.pre, bf16[256,2304]{1,0:T(8,128)(2,1)S(1)} %copy-done, ...), custom_call_target="tpu_custom_call", output_to_operand_aliasing={{0}: (6, {})} | custom-call | tf_op jit(solution)/shard_map/last_products/pallas_call | solution.py:344
Async XLA Ops:
  2.3 10.3 %collective-permute-start = (bf16[128,1152]{1,0:T(8,128)(2,1)S(1)}, bf16[128,1152]{1,0:T(8,128)(2,1)S(1)}, u32[]{:S(2)}, u32[]{:S(2)}) collective-permute-start(bf16[128,1152]{1,0:T(8,128)(2,1)S(1)} %get-tuple-element.14), channel_id=1, source_target_pairs={{0,32},{32,0},{1,33},{33,1},{2,34},{34,2},{3,35},{35,3},{4,36},{36... | collective-permute-start | bytes 884744 | tf_op jit(solution)/shard_map/ppermute | solution.py:375
  46.2 21.7 %copy-start = (bf16[256,2304]{1,0:T(8,128)(2,1)S(1)}, bf16[256,2304]{1,0:T(8,128)(2,1)}, u32[]{:S(2)}) copy-start(bf16[256,2304]{1,0:T(8,128)(2,1)} %weight.3) | copy-start | bytes 3538948
  63.2 6.3 %collective-permute-start.1 = (bf16[128,2304]{1,0:T(8,128)(2,1)S(1)}, bf16[128,2304]{1,0:T(8,128)(2,1)S(1)}, u32[]{:S(2)}, u32[]{:S(2)}) collective-permute-start(bf16[128,2304]{1,0:T(8,128)(2,1)S(1)} %bitcast.1), channel_id=1, source_target_pairs={{0,32},{32,0},{1,33},{33,1},{2,34},{34,2},{3,35},{35,3},{4,36},{36... | collective-permute-start | bytes 1769480 | tf_op jit(solution)/shard_map/ppermute | solution.py:385

commit v8 on v7

--- a/solution.py
+++ b/solution.py
@@ -8,7 +8,7 @@
 from jax.sharding import Mesh, PartitionSpec as P
 
 BF16, F32 = jnp.bfloat16, jnp.float32
-LANES, SUBLANES, CHUNKS = 128, 8, 3
+LANES, SUBLANES, CHUNKS, PARTS = 128, 8, 3, 1
 AXES = ("x", "yh", "core", "ya", "yb", "za", "zb")
 SIZES = (4, 2, 2, 2, 2, 4, 2)
 NEAR, FAR = ("x", "yb", "zb"), ("yh", "ya", "za")
@@ -77,11 +77,11 @@
     batch, half = out.shape
     piece, width = strip.shape[0], bias.shape[0]
     rows, columns = inputs.shape
-    step = half // CHUNKS
+    step = half // PARTS
     x, yh, core, ya, yb, za, zb = (lax.axis_index(a) for a in AXES)
     there = (1 - core) * half
     pairs = [(inputs_hbm, inputs), (bias_hbm, bias), (pre_hbm, pre)]
-    for i in range(CHUNKS):
+    for i in range(PARTS):
         columns_there = pl.ds(pl.multiple_of(there + i * step, LANES), step)
         pairs.append((weight_hbm.at[:, columns_there], weight.at[:, pl.ds(i * step, step)]))
     copies = [pltpu.make_async_copy(a, b, sems.at[i]) for i, (a, b) in enumerate(pairs)]
@@ -104,7 +104,7 @@
     ordered[...] = dot(order, pre[...], (1, 0)).astype(BF16)
     hidden = jnp.maximum(ordered[...], jnp.zeros_like(ordered[...]))
     place = jnp.where(first // half == core, batch, own_place(ya, yb, za, zb))
-    for i in range(CHUNKS):
+    for i in range(PARTS):
         copies[3 + i].wait()
         part = pl.ds(i * step, step)
         product = dot(hidden, weight[:, part], (1, 0))
@@ -137,7 +137,7 @@
             pltpu.VMEM((weight.shape[0], half), BF16),
             pltpu.VMEM(inputs.shape, BF16),
             pltpu.VMEM(bias.shape, F32),
-            pltpu.SemaphoreType.DMA((3 + CHUNKS,)),
+            pltpu.SemaphoreType.DMA((3 + PARTS,)),
         ],
         compiler_params=pltpu.CompilerParams(vmem_limit_bytes=12 << 20),
         name="first_product",
@@ -245,7 +245,9 @@
     return jnp.concatenate(part, axis=0)
 
 
-def near_kernel(tail, own, pre, weight, decoder_out, backward, turned, flipped, decoder, sems):
+def near_kernel(
+    tail, own, pre, weight, decoder_out, backward, turned, flipped, crossed, decoder, sems
+):
     features, half = decoder.shape
     core = lax.axis_index("core")
     xs, size = lax.axis_size("x"), lax.axis_size("yh") * LANES
@@ -263,6 +265,7 @@
     for x in range(xs):
         turned[x * size : (x + 1) * size, :] = block_rows(own, x, half).T
     turned[xs * size :, :] = tail_rows(own, half, tail).T
+    crossed[...] = weight[:, pl.ds(pl.multiple_of((1 - core) * half, LANES), half)].T
     for copy in copies:
         copy.wait()
 
@@ -278,9 +281,10 @@
             pltpu.VMEM(pre.shape, F32),
             pltpu.VMEM((half, batch), BF16),
             pltpu.VMEM((features, batch), BF16),
+            pltpu.VMEM((half, features), BF16),
         ),
         in_specs=[VMEM] * 3,
-        out_specs=(pl.BlockSpec(memory_space=pltpu.HBM), VMEM, VMEM, VMEM),
+        out_specs=(pl.BlockSpec(memory_space=pltpu.HBM),) + (VMEM,) * 4,
         scratch_shapes=[pltpu.VMEM((features, half), BF16), pltpu.SemaphoreType.DMA((2,))],
         compiler_params=pltpu.CompilerParams(vmem_limit_bytes=10 << 20),
         cost_estimate=pl.CostEstimate(
@@ -293,7 +297,7 @@
 
 
 def last_kernel(
-    tail, other, pre, weight, backward, turned, flipped, _, decoder_out, encoder_out, decoder, encoder, sems
+    tail, other, pre, backward, turned, flipped, crossed, _, decoder_out, encoder_out, decoder, encoder, sems
 ):
     half = decoder.shape[1]
     core = lax.axis_index("core")
@@ -307,7 +311,7 @@
 
     columns = pl.ds(pl.multiple_of((1 - core) * half, LANES), half)
     residual = other[:, :half]
-    total = backward[...] + dot(residual, weight[:, columns], (1, 1))
+    total = backward[...] + dot(residual, crossed[...], (1, 0))
     masked = jnp.where(pre[...] > 0, total, jnp.zeros_like(total)).astype(BF16)
     decoder[...] = dot(flipped[...], residual, (1, 0)).astype(BF16)
     send(decoder, decoder_out.at[:, columns])
@@ -337,9 +341,9 @@
         copy.wait()
 
 
-def last_products(other, pre, weight, near, tail):
+def last_products(other, pre, near, tail):
     decoder, *rest = near
-    features, width = weight.shape
+    features, width = decoder.shape
     raw = pl.BlockSpec(memory_space=pltpu.HBM)
     return pl.pallas_call(
         functools.partial(last_kernel, tail),
@@ -357,7 +361,7 @@
         input_output_aliases={6: 0},
         compiler_params=pltpu.CompilerParams(vmem_limit_bytes=20 << 20),
         name="last_products",
-    )(other, pre, weight, *rest, decoder)
+    )(other, pre, *rest, decoder)
 
 
 def shards(inputs, decoder_bias, preactivations, decoder_weight):
@@ -384,7 +388,7 @@
     own = swap(own, ("x", *PLANE), near_groups()).reshape(batch, width)
     other = lax.ppermute(own, "core", partner)
     near_part = near_products(own, ordered, decoder_weight, tail)
-    grad_decoder, grad_encoder = last_products(other, ordered, decoder_weight, near_part, tail)
+    grad_decoder, grad_encoder = last_products(other, ordered, near_part, tail)
     return (grad_encoder, grad_decoder)
 
 

time: 71.7 us -> 71.3 us (level)
  no operation moved by 1% of the time
where the time goes in v8:
time: 71.3 us; the launch traced here: 71 us
  blocking collectives  50.3 us (71%)
  starting transfers between devices  13.4 us (19%)
  Pallas kernels  6.07 us (9%)
    all_to_all x3, blocking collectives, swap(): lax.all_to_all(x, axis, split_axis=0, concat_axis=0, axis_index_groups=gr...  50.3 us
    ppermute x1, starting transfers between devices, shards(): arrived = lax.ppermute(theirs, 'core', partner)  8.75 us
    ppermute x1, starting transfers between devices, shards(): other = lax.ppermute(own, 'core', partner)  4.66 us
    pallas_call x1, Pallas kernels, last_products(): pl.pallas_call(functools.partial(last_kernel, tail), out_shape=(jax.Shape...  1.75 us
    pallas_call x1, Pallas kernels, own_product(): pl.pallas_call(own_kernel, out_shape=pltpu.VMEM((batch, half), F32), in_s...  1.54 us
    pallas_call x1, Pallas kernels, first_product(): pl.pallas_call(first_kernel, out_shape=(pltpu.VMEM((pre.shape[0], half),...  1.44 us
  transfers between devices with their start and end apart: 2, of which 1 were waited for; matrix products, arithmetic and copies ran while one was open for 0% of the time, Pallas kernels for 4%

profile of v8, /device:TPU:1, one launch (start us, length us, event | category | flops | bytes accessed | tf_op | source)
XLA Modules:
  0.0 71.0 jit_solution(1471101788961124950)
XLA Ops:
  0.6 1.4 %first_product.1 = (bf16[128,1152]{1,0:T(8,128)(2,1)S(1)}, bf16[128,256]{1,0:T(8,128)(2,1)S(1)}, bf16[8,128]{1,0:T(8,128)(2,1)S(1)}, f32[8,1152]{1,0:T(8,128)S(1)}) custom-call(bf16[128,256]{1,0:T(8,128)(2,1)} %pre_hbm.1, bf16[256,2304]{1,0:T(8,128)(2,1)} %weight.1, bf16[4,144]{1,0:T(4,128)(2,1)} %inputs_hbm.1, f32[2304]{0:T(1024)} %bias_hbm.1), custom_call_target="tpu_custom_call" | custom-call | tf_op jit(solution)/shard_map/first_product/pallas_call | solution.py:125
  2.1 8.7 %collective-permute-start = (bf16[128,1152]{1,0:T(8,128)(2,1)S(1)}, bf16[128,1152]{1,0:T(8,128)(2,1)S(1)}, u32[]{:S(2)}, u32[]{:S(2)}) collective-permute-start(bf16[128,1152]{1,0:T(8,128)(2,1)S(1)} %get-tuple-element.15), channel_id=1, source_target_pairs={{0,32},{32,0},{1,33},{33,1},{2,34},{34,2},{3,35},{35,3},{4,36},{36... | collective-permute-start | bytes 884744 | tf_op jit(solution)/shard_map/ppermute | solution.py:379
  10.8 1.5 %own_product.1.own = f32[128,1152]{1,0:T(8,128)S(1)} custom-call(bf16[128,256]{1,0:T(8,128)(2,1)S(1)} %get-tuple-element.13.ordered.pre, f32[8,1152]{1,0:T(8,128)S(1)} %get-tuple-element.14.strip, bf16[256,2304]{1,0:T(8,128)(2,1)} %weight.1), custom_call_target="tpu_custom_call" | custom-call | flops 75497472 | bytes 589824 | tf_op jit(solution)/shard_map/own_product/pallas_call | solution.py:169
  12.4 0.0 collective-permute-done.arrived
  12.4 0.1 join_cores.1
  12.5 10.2 %all_to_all.15.arrived = bf16[16,8,1152]{2,1,0:T(8,128)(2,1)S(1)} all-to-all(bf16[16,8,1152]{2,1,0:T(8,128)(2,1)S(1)} %join_cores.1), channel_id=1, replica_groups={{0,1,8,9,128,129,136,137,256,257,264,265,384,385,392,393},{3,2,11,10,13..., dimensions={0} | all-to-all | bytes 589824 | tf_op jit(solution)/shard_map/all_to_all | solution.py:34
  22.7 0.1 second_sum.1
  22.7 24.2 %all_to_all.16.arrived = bf16[16,8,1280]{2,1,0:T(8,128)(2,1)S(1)} all-to-all(bf16[16,8,1280]{2,1,0:T(8,128)(2,1)S(1)} %second_sum.1), channel_id=1, replica_groups={{0,3,5,6,24,27,29,30,72,75,77,78,80,83,85,86},{1,2,4,7,25,26,28,31,73,7..., dimensions={0} | all-to-all | bytes 655360 | tf_op jit(solution)/shard_map/all_to_all | solution.py:34
  46.9 0.0 copy-start
  46.9 0.1 third_sum.1
  47.0 15.9 %all_to_all.17 = bf16[16,8,2304]{2,1,0:T(8,128)(2,1)S(1)} all-to-all(bf16[16,8,2304]{2,1,0:T(8,128)(2,1)S(1)} %third_sum.1), channel_id=1, replica_groups={{0,1,8,9,128,129,136,137,256,257,264,265,384,385,392,393},{3,2,11,10,13..., dimensions={0} | all-to-all | bytes 1179648 | tf_op jit(solution)/shard_map/all_to_all | solution.py:34
  62.9 4.7 %collective-permute-start.1 = (bf16[128,2304]{1,0:T(8,128)(2,1)S(1)}, bf16[128,2304]{1,0:T(8,128)(2,1)S(1)}, u32[]{:S(2)}, u32[]{:S(2)}) collective-permute-start(bf16[128,2304]{1,0:T(8,128)(2,1)S(1)} %bitcast.1), channel_id=1, source_target_pairs={{0,32},{32,0},{1,33},{33,1},{2,34},{34,2},{3,35},{35,3},{4,36},{36... | collective-permute-start | bytes 1769480 | tf_op jit(solution)/shard_map/ppermute | solution.py:389
  67.6 0.0 copy-done
  67.6 1.1 %near_products.1 = (bf16[256,2304]{1,0:T(8,128)(2,1)}, f32[128,256]{1,0:T(8,128)S(1)}, bf16[1152,128]{1,0:T(8,128)(2,1)S(1)}, bf16[256,128]{1,0:T(8,128)(2,1)S(1)}, bf16[1152,256]{1,0:T(8,128)(2,1)S(1)}) custom-call(bf16[128,2304]{1,0:T(8,128)(2,1)S(1)} %bitcast.2, bf16[128,256]{1,0:T(8,128)(2,1)S(1)} %get-tuple-element.13.ordered.pre, ...), custom_call_target="tpu_custom_call" | custom-call | flops 150994944 | bytes 1179648 | tf_op jit(solution)/shard_map/near_products/pallas_call | solution.py:277
  68.8 0.5 collective-permute-done.1.other
  69.2 1.8 %last_products.1 = (bf16[256,2304]{1,0:T(8,128)(2,1)}, bf16[2304,256]{1,0:T(8,128)(2,1)}) custom-call(bf16[128,2304]{1,0:T(8,128)(2,1)S(1)} %collective-permute-done.1.other, bf16[128,256]{1,0:T(8,128)(2,1)S(1)} %get-tuple-element.13.ordered.pre, f32[128,256]{1,0:T(8,128)S(1)} %get-tuple-element.17.backward, ...), custom_call_target="tpu_custom_call", output_to_operand_aliasing={{0}: (6, {})} | custom-call | tf_op jit(solution)/shard_map/last_products/pallas_call | solution.py:348
Async XLA Ops:
  2.1 10.3 %collective-permute-start = (bf16[128,1152]{1,0:T(8,128)(2,1)S(1)}, bf16[128,1152]{1,0:T(8,128)(2,1)S(1)}, u32[]{:S(2)}, u32[]{:S(2)}) collective-permute-start(bf16[128,1152]{1,0:T(8,128)(2,1)S(1)} %get-tuple-element.15), channel_id=1, source_target_pairs={{0,32},{32,0},{1,33},{33,1},{2,34},{34,2},{3,35},{35,3},{4,36},{36... | collective-permute-start | bytes 884744 | tf_op jit(solution)/shard_map/ppermute | solution.py:379
  46.9 20.7 %copy-start = (bf16[256,2304]{1,0:T(8,128)(2,1)S(1)}, bf16[256,2304]{1,0:T(8,128)(2,1)}, u32[]{:S(2)}) copy-start(bf16[256,2304]{1,0:T(8,128)(2,1)} %weight.1) | copy-start | bytes 3538948
  62.9 6.3 %collective-permute-start.1 = (bf16[128,2304]{1,0:T(8,128)(2,1)S(1)}, bf16[128,2304]{1,0:T(8,128)(2,1)S(1)}, u32[]{:S(2)}, u32[]{:S(2)}) collective-permute-start(bf16[128,2304]{1,0:T(8,128)(2,1)S(1)} %bitcast.1), channel_id=1, source_target_pairs={{0,32},{32,0},{1,33},{33,1},{2,34},{34,2},{3,35},{35,3},{4,36},{36... | collective-permute-start | bytes 1769480 | tf_op jit(solution)/shard_map/ppermute | solution.py:389

commit v9 on v8

--- a/solution.py
+++ b/solution.py
@@ -8,7 +8,7 @@
 from jax.sharding import Mesh, PartitionSpec as P
 
 BF16, F32 = jnp.bfloat16, jnp.float32
-LANES, SUBLANES, CHUNKS, PARTS = 128, 8, 3, 1
+LANES, SUBLANES, CHUNKS, PARTS = 128, 8, 1, 1
 AXES = ("x", "yh", "core", "ya", "yb", "za", "zb")
 SIZES = (4, 2, 2, 2, 2, 4, 2)
 NEAR, FAR = ("x", "yb", "zb"), ("yh", "ya", "za")
@@ -250,7 +250,7 @@
 ):
     features, half = decoder.shape
     core = lax.axis_index("core")
-    xs, size = lax.axis_size("x"), lax.axis_size("yh") * LANES
+    xs = lax.axis_size("x")
     flipped[...] = jnp.maximum(pre[...], jnp.zeros_like(pre[...])).T
     columns = pl.ds(pl.multiple_of(core * half, LANES), half)
     copies = []
@@ -263,8 +263,10 @@
         copies[-1].start()
     backward[...] = dot(own[:, :half], weight[:, columns], (1, 1))
     for x in range(xs):
-        turned[x * size : (x + 1) * size, :] = block_rows(own, x, half).T
-    turned[xs * size :, :] = tail_rows(own, half, tail).T
+        block = block_rows(own, x, half).T
+        turned[x * LANES : (x + 1) * LANES, :] = block[:LANES]
+        turned[half - (xs - x) * LANES : half - (xs - x - 1) * LANES, :] = block[LANES:]
+    turned[xs * LANES : (xs + 1) * LANES, :] = tail_rows(own, half, tail).T
     crossed[...] = weight[:, pl.ds(pl.multiple_of((1 - core) * half, LANES), half)].T
     for copy in copies:
         copy.wait()
@@ -302,7 +304,7 @@
     half = decoder.shape[1]
     core = lax.axis_index("core")
     cores, xs, yhs = (lax.axis_size(a) for a in ("core", "x", "yh"))
-    span, size = LANES + tail, yhs * LANES
+    span = LANES + tail
     copies = []
 
     def send(source, target):
@@ -318,25 +320,24 @@
     depth = masked.shape[0] // (2 * lax.axis_size("za"))
     swapped = [masked[(i ^ 1) * depth : ((i ^ 1) + 1) * depth] for i in range(masked.shape[0] // depth)]
     met = (masked, jnp.concatenate(swapped, axis=0))
+    theirs = [block_rows(other, x, half) for x in range(xs)]
     other_tails = tail_rows(other, half, tail)
-    own_ends = [dot(turned[xs * size :, :], m, (1, 0)).astype(BF16) for m in met]
-    other_ends = [dot(other_tails, m, (0, 0)).astype(BF16) for m in met]
-    for x in range(xs):
-        theirs = block_rows(other, x, half)
-        for yh, m in enumerate(met):
-            first = x * size + yh * LANES
-            own_block = dot(turned[first : first + LANES, :], m, (1, 0)).astype(BF16)
-            other_block = dot(theirs[:, yh * LANES : (yh + 1) * LANES], m, (0, 0)).astype(BF16)
-            end = (x * yhs + yh) * tail
-            for block, ends, c in (
-                (own_block, own_ends[yh], core),
-                (other_block, other_ends[yh], 1 - core),
-            ):
+    for yh, m in enumerate(met):
+        first = yh * xs * LANES
+        lanes = [t[:, yh * LANES : (yh + 1) * LANES] for t in theirs]
+        lanes = lanes + [other_tails] if yh == 0 else [other_tails] + lanes
+        blocks = (
+            (dot(turned[first : first + (xs + 1) * LANES, :], m, (1, 0)).astype(BF16), core),
+            (dot(jnp.concatenate(lanes, axis=1), m, (0, 0)).astype(BF16), 1 - core),
+        )
+        for block, c in blocks:
+            for x in range(xs):
+                at = (x + yh) * LANES
+                end = (0 if yh else xs * LANES) + (x * yhs + yh) * tail
                 start = pl.multiple_of(((x * yhs + yh) * cores + c) * span, tail)
-                encoder[pl.ds(start, LANES), :] = block
-                encoder[pl.ds(pl.multiple_of(start + LANES, tail), tail), :] = ends[end : end + tail]
-        rows = pl.ds(x * yhs * cores * span, yhs * cores * span)
-        send(encoder.at[rows], encoder_out.at[rows])
+                encoder[pl.ds(start, LANES), :] = block[at : at + LANES]
+                encoder[pl.ds(pl.multiple_of(start + LANES, tail), tail), :] = block[end : end + tail]
+                send(encoder.at[pl.ds(start, span)], encoder_out.at[pl.ds(start, span)])
     for copy in copies:
         copy.wait()
 
@@ -356,7 +357,7 @@
         scratch_shapes=[
             pltpu.VMEM((features, width // lax.axis_size("core")), BF16),
             pltpu.VMEM((width, features), BF16),
-            pltpu.SemaphoreType.DMA((1 + lax.axis_size("x"),)),
+            pltpu.SemaphoreType.DMA((1 + width // (LANES + tail),)),
         ],
         input_output_aliases={6: 0},
         compiler_params=pltpu.CompilerParams(vmem_limit_bytes=20 << 20),

time: 71.3 us -> 70.9 us (level)
  no operation moved by 1% of the time
where the time goes in v9:
time: 70.9 us; the launch traced here: 70.6 us
  blocking collectives  49.7 us (70%)
  starting transfers between devices  13.9 us (20%)
  Pallas kernels  5.89 us (8%)
    all_to_all x3, blocking collectives, swap(): lax.all_to_all(x, axis, split_axis=0, concat_axis=0, axis_index_groups=gr...  49.7 us
    ppermute x1, starting transfers between devices, shards(): arrived = lax.ppermute(theirs, 'core', partner)  8.75 us
    ppermute x1, starting transfers between devices, shards(): other = lax.ppermute(own, 'core', partner)  5.11 us
    pallas_call x1, Pallas kernels, last_products(): pl.pallas_call(functools.partial(last_kernel, tail), out_shape=(jax.Shape...  1.76 us
    pallas_call x1, Pallas kernels, first_product(): pl.pallas_call(first_kernel, out_shape=(pltpu.VMEM((pre.shape[0], half),...  1.44 us
  transfers between devices with their start and end apart: 2, of which 1 were waited for; matrix products, arithmetic and copies ran while one was open for 0% of the time, Pallas kernels for 4%

profile of v9, /device:TPU:1, one launch (start us, length us, event | category | flops | bytes accessed | tf_op | source)
XLA Modules:
  0.0 70.6 jit_solution(10930281057850705878)
XLA Ops:
  0.6 1.4 %first_product.1 = (bf16[128,1152]{1,0:T(8,128)(2,1)S(1)}, bf16[128,256]{1,0:T(8,128)(2,1)S(1)}, bf16[8,128]{1,0:T(8,128)(2,1)S(1)}, f32[8,1152]{1,0:T(8,128)S(1)}) custom-call(bf16[128,256]{1,0:T(8,128)(2,1)} %pre_hbm.1, bf16[256,2304]{1,0:T(8,128)(2,1)} %weight.1, bf16[4,144]{1,0:T(4,128)(2,1)} %inputs_hbm.1, f32[2304]{0:T(1024)} %bias_hbm.1), custom_call_target="tpu_custom_call" | custom-call | tf_op jit(solution)/shard_map/first_product/pallas_call | solution.py:125
  2.1 8.7 %collective-permute-start = (bf16[128,1152]{1,0:T(8,128)(2,1)S(1)}, bf16[128,1152]{1,0:T(8,128)(2,1)S(1)}, u32[]{:S(2)}, u32[]{:S(2)}) collective-permute-start(bf16[128,1152]{1,0:T(8,128)(2,1)S(1)} %get-tuple-element.15), channel_id=1, source_target_pairs={{0,32},{32,0},{1,33},{33,1},{2,34},{34,2},{3,35},{35,3},{4,36},{36... | collective-permute-start | bytes 884744 | tf_op jit(solution)/shard_map/ppermute | solution.py:380
  10.8 1.3 %own_product.1.own = f32[128,1152]{1,0:T(8,128)S(1)} custom-call(bf16[128,256]{1,0:T(8,128)(2,1)S(1)} %get-tuple-element.13.ordered.pre, f32[8,1152]{1,0:T(8,128)S(1)} %get-tuple-element.14.strip, bf16[256,2304]{1,0:T(8,128)(2,1)} %weight.1), custom_call_target="tpu_custom_call" | custom-call | flops 75497472 | bytes 589824 | tf_op jit(solution)/shard_map/own_product/pallas_call | solution.py:169
  12.2 0.0 collective-permute-done.arrived
  12.2 0.1 join_cores.1
  12.3 9.9 %all_to_all.15.arrived = bf16[16,8,1152]{2,1,0:T(8,128)(2,1)S(1)} all-to-all(bf16[16,8,1152]{2,1,0:T(8,128)(2,1)S(1)} %join_cores.1), channel_id=1, replica_groups={{0,1,8,9,128,129,136,137,256,257,264,265,384,385,392,393},{3,2,11,10,13..., dimensions={0} | all-to-all | bytes 589824 | tf_op jit(solution)/shard_map/all_to_all | solution.py:34
  22.1 0.1 second_sum.1
  22.2 23.6 %all_to_all.16.arrived = bf16[16,8,1280]{2,1,0:T(8,128)(2,1)S(1)} all-to-all(bf16[16,8,1280]{2,1,0:T(8,128)(2,1)S(1)} %second_sum.1), channel_id=1, replica_groups={{0,3,5,6,24,27,29,30,72,75,77,78,80,83,85,86},{1,2,4,7,25,26,28,31,73,7..., dimensions={0} | all-to-all | bytes 655360 | tf_op jit(solution)/shard_map/all_to_all | solution.py:34
  45.8 0.0 copy-start
  45.8 0.1 third_sum.1
  45.9 16.2 %all_to_all.17 = bf16[16,8,2304]{2,1,0:T(8,128)(2,1)S(1)} all-to-all(bf16[16,8,2304]{2,1,0:T(8,128)(2,1)S(1)} %third_sum.1), channel_id=1, replica_groups={{0,1,8,9,128,129,136,137,256,257,264,265,384,385,392,393},{3,2,11,10,13..., dimensions={0} | all-to-all | bytes 1179648 | tf_op jit(solution)/shard_map/all_to_all | solution.py:34
  62.1 5.1 %collective-permute-start.1 = (bf16[128,2304]{1,0:T(8,128)(2,1)S(1)}, bf16[128,2304]{1,0:T(8,128)(2,1)S(1)}, u32[]{:S(2)}, u32[]{:S(2)}) collective-permute-start(bf16[128,2304]{1,0:T(8,128)(2,1)S(1)} %bitcast.1), channel_id=1, source_target_pairs={{0,32},{32,0},{1,33},{33,1},{2,34},{34,2},{3,35},{35,3},{4,36},{36... | collective-permute-start | bytes 1769480 | tf_op jit(solution)/shard_map/ppermute | solution.py:390
  67.2 0.0 copy-done
  67.3 1.1 %near_products.1 = (bf16[256,2304]{1,0:T(8,128)(2,1)}, f32[128,256]{1,0:T(8,128)S(1)}, bf16[1152,128]{1,0:T(8,128)(2,1)S(1)}, bf16[256,128]{1,0:T(8,128)(2,1)S(1)}, bf16[1152,256]{1,0:T(8,128)(2,1)S(1)}) custom-call(bf16[128,2304]{1,0:T(8,128)(2,1)S(1)} %bitcast.2, bf16[128,256]{1,0:T(8,128)(2,1)S(1)} %get-tuple-element.13.ordered.pre, ...), custom_call_target="tpu_custom_call" | custom-call | flops 150994944 | bytes 1179648 | tf_op jit(solution)/shard_map/near_products/pallas_call | solution.py:279
  68.4 0.5 collective-permute-done.1.other
  68.9 1.8 %last_products.1 = (bf16[256,2304]{1,0:T(8,128)(2,1)}, bf16[2304,256]{1,0:T(8,128)(2,1)}) custom-call(bf16[128,2304]{1,0:T(8,128)(2,1)S(1)} %collective-permute-done.1.other, bf16[128,256]{1,0:T(8,128)(2,1)S(1)} %get-tuple-element.13.ordered.pre, f32[128,256]{1,0:T(8,128)S(1)} %get-tuple-element.17.backward, ...), custom_call_target="tpu_custom_call", output_to_operand_aliasing={{0}: (6, {})} | custom-call | tf_op jit(solution)/shard_map/last_products/pallas_call | solution.py:349
Async XLA Ops:
  2.1 10.1 %collective-permute-start = (bf16[128,1152]{1,0:T(8,128)(2,1)S(1)}, bf16[128,1152]{1,0:T(8,128)(2,1)S(1)}, u32[]{:S(2)}, u32[]{:S(2)}) collective-permute-start(bf16[128,1152]{1,0:T(8,128)(2,1)S(1)} %get-tuple-element.15), channel_id=1, source_target_pairs={{0,32},{32,0},{1,33},{33,1},{2,34},{34,2},{3,35},{35,3},{4,36},{36... | collective-permute-start | bytes 884744 | tf_op jit(solution)/shard_map/ppermute | solution.py:380
  45.8 21.5 %copy-start = (bf16[256,2304]{1,0:T(8,128)(2,1)S(1)}, bf16[256,2304]{1,0:T(8,128)(2,1)}, u32[]{:S(2)}) copy-start(bf16[256,2304]{1,0:T(8,128)(2,1)} %weight.1) | copy-start | bytes 3538948
  62.1 6.7 %collective-permute-start.1 = (bf16[128,2304]{1,0:T(8,128)(2,1)S(1)}, bf16[128,2304]{1,0:T(8,128)(2,1)S(1)}, u32[]{:S(2)}, u32[]{:S(2)}) collective-permute-start(bf16[128,2304]{1,0:T(8,128)(2,1)S(1)} %bitcast.1), channel_id=1, source_target_pairs={{0,32},{32,0},{1,33},{33,1},{2,34},{34,2},{3,35},{35,3},{4,36},{36... | collective-permute-start | bytes 1769480 | tf_op jit(solution)/shard_map/ppermute | solution.py:390
